TPU v7x, 32 devices: a whole 2x2x4 slice. The times are simulated.
32 devices in a mesh: col: 16 (over z, x, core), orb: 2 (over y).
Axes of the slice: x: 2, y: 2, z: 4, core: 2. Of those that a mesh axis runs over, the one named last changes fastest.
Arguments:
- slab_occ: bfloat16 [1024, 400], P('col', 'orb'), may hold values from -6 to 6
- slab_vir: bfloat16 [1024, 2400], P('col', 'orb'), may hold values from -6 to 6
- orbitals_occ: bfloat16 [400, 16384], P('orb', 'col'), may hold values from -0.3125 to 0.3125
- orbitals_vir: bfloat16 [2400, 16384], P('orb', 'col'), may hold values from -0.125 to 0.125
- occ_energy: float32 [400], P('orb'), may hold values from -2 to -0.1
- vir_energy: float32 [2400], P('orb'), may hold values from 0.1 to 3
- screened: bfloat16 [1024, 16384], P('col'), may hold values from -6 to 6
Outputs:
- occ_kernel: bfloat16 [1024, 400], P(('col', 'orb'))
- vir_kernel: bfloat16 [1024, 2400], P(('col', 'orb'))
All inputs are finite; a program needn't handle non-finite values.
Results may differ from a plain program's by a relative error of at most 0.014.
Values may be sent and summed in bfloat16 or wider, within the bound.
A program may use at most 64 MiB of HBM per device.

v0:
```python
import functools

import jax
import jax.numpy as jnp
from jax import lax
from jax.experimental import pallas as pl
from jax.experimental.pallas import tpu as pltpu
from jax.sharding import PartitionSpec as P

MESH = pl.DeviceIdType.MESH
LAGS = (1, 2)
ANY = pl.BlockSpec(memory_space=pl.ANY)
VMEM = pl.BlockSpec(memory_space=pltpu.VMEM)


def place(n_col):
    me = lax.axis_index("col")
    far, mid, core = me // 4, lax.rem(me // 2, 2), lax.rem(me, 2)
    return me, far, mid, core, lambda f, m, c: (f * 2 + m) * 2 + c


def greet(cols, orbs):
    barrier = pltpu.get_barrier_semaphore()
    for col in cols:
        pl.semaphore_signal(barrier, inc=1, device_id={"col": col}, device_id_type=MESH)
    for orb in orbs:
        pl.semaphore_signal(barrier, inc=1, device_id={"orb": orb}, device_id_type=MESH)
    pl.semaphore_wait(barrier, len(cols) + len(orbs))


def sender():
    sends = []

    def push(src, dst, send, recv, device):
        copy = pltpu.make_async_remote_copy(
            src_ref=src, dst_ref=dst, send_sem=send, recv_sem=recv,
            device_id=device, device_id_type=MESH,
        )
        copy.start()
        sends.append(copy)
        return copy

    return sends, push


def landed(ref, send, recv, device):
    pltpu.make_async_remote_copy(
        src_ref=ref, dst_ref=ref, send_sem=send, recv_sem=recv,
        device_id=device, device_id_type=MESH,
    ).wait_recv()


def spread(n_col, push, swap, slab, screen, slabs, screens, local_sem,
           orb_send, slab_send, slab_recv, screen_send, screen_recv):
    n_far = n_col // 4
    me, far, mid, core, index = place(n_col)
    part = lax.axis_index("orb")
    other = 1 - part
    others = [lax.rem(me + d, n_col) for d in range(1, n_col)]

    def arrived(k, col):
        landed(slabs.at[k, col], orb_send.at[swap], slab_recv.at[k, col], {"orb": other})

    counter = [0]

    def give(k, col, target, src=None):
        push(
            slabs.at[k, col] if src is None else src, slabs.at[k, col],
            slab_send.at[counter[0]], slab_recv.at[k, col], {"col": target},
        )
        counter[0] += 1

    x_peer, core_peer = index(far, 1 - mid, core), index(far, mid, 1 - core)
    fars = [lax.rem(far + d, n_far) for d in range(1, n_far)]
    own = slab.at[part]
    targets = [index(f, mid, core) for f in fars] + [x_peer, core_peer]
    for target in targets:
        give(0, me, target, own)
    arrived(1, me)
    for target in targets:
        give(1, me, target)
    for n, p in enumerate(others):
        push(screen.at[p], screens.at[me], screen_send.at[n], screen_recv.at[me], {"col": p})
    local = [
        pltpu.make_async_copy(own, slabs.at[0, me], local_sem.at[0]),
        pltpu.make_async_copy(screen.at[me], screens.at[me], local_sem.at[1]),
    ]
    for copy in local:
        copy.start()
    for f in fars:
        col = index(f, mid, core)
        for k in range(2):
            arrived(k, col)
            give(k, col, x_peer)
            give(k, col, core_peer)
    for f in [far] + fars:
        col = index(f, 1 - mid, core)
        for k in range(2):
            arrived(k, col)
            give(k, col, core_peer)
    for f in [far] + fars:
        for m in (mid, 1 - mid):
            for k in range(2):
                arrived(k, index(f, m, 1 - core))
    for p in others:
        landed(screens.at[p], orb_send.at[swap], screen_recv.at[p], {"orb": other})
    for copy in local:
        copy.wait()


def spread_semaphores(n_col):
    n_far = n_col // 4
    dma = pltpu.SemaphoreType.DMA
    n_give = 2 * ((n_far + 1) + 2 * (n_far - 1) + n_far)
    return [dma((n_give,)), dma((2, n_col)), dma((n_col,)), dma((n_col,))]


def gather_kernel(
    n_col, slab, occ, vir, screen, slabs, peer_occ, peer_vir, screens,
    local_sem, orb_send, orb_recv, slab_send, slab_recv, screen_send, screen_recv,
):
    me = lax.axis_index("col")
    other = 1 - lax.axis_index("orb")
    greet([lax.rem(me + d, n_col) for d in range(1, n_col)], [other])
    sends, push = sender()
    push(slab.at[other], slabs.at[1, me], orb_send.at[2], slab_recv.at[1, me], {"orb": other})
    push(vir, peer_vir, orb_send.at[0], orb_recv.at[0], {"orb": other})
    push(occ, peer_occ, orb_send.at[1], orb_recv.at[1], {"orb": other})
    spread(n_col, push, 2, slab, screen, slabs, screens, local_sem,
           orb_send, slab_send, slab_recv, screen_send, screen_recv)
    for n, ref in ((0, peer_vir), (1, peer_occ)):
        landed(ref, orb_send.at[n], orb_recv.at[n], {"orb": other})
    for copy in sends:
        copy.wait_send()


def gather(n_col, slab, occ, vir, screen):
    dma = pltpu.SemaphoreType.DMA
    return pl.pallas_call(
        functools.partial(gather_kernel, n_col),
        out_shape=(
            jax.ShapeDtypeStruct((2, n_col) + slab.shape[1:], slab.dtype),
            jax.ShapeDtypeStruct(occ.shape, occ.dtype),
            jax.ShapeDtypeStruct(vir.shape, vir.dtype),
            jax.ShapeDtypeStruct(screen.shape, screen.dtype),
        ),
        in_specs=[ANY] * 4,
        out_specs=(ANY,) * 4,
        scratch_shapes=[dma((2,)), dma((3,)), dma((2,))] + spread_semaphores(n_col),
        compiler_params=pltpu.CompilerParams(collective_id=0, has_side_effects=True),
    )(slab, occ, vir, screen)


def reduce_rows(n_col, pieces, ins, refs, ready, finish, flush=()):
    n_far = n_col // 4
    near, out_x, in_x, total, out_far, in_far = [
        refs[i * pieces : (i + 1) * pieces] for i in range(6)
    ]
    near_send, near_recv, x_send, x_recv, far_send, far_recv = refs[6 * pieces :]
    me, far, mid, core, index = place(n_col)
    x_peer, core_peer = index(far, 1 - mid, core), index(far, mid, 1 - core)
    fars = [lax.rem(far + d, n_far) for d in range(1, n_far)]
    sends, push = sender()
    wide = lambda value: value.astype(jnp.float32)
    first, second, third = [], [], []

    def to_core(t):
        ready(t)
        first.append(
            [
                push(
                    ins[t].at[:, m, 1 - core], near[t].at[slot],
                    near_send.at[t, slot], near_recv.at[t, slot], {"col": core_peer},
                )
                for slot, m in ((0, 1 - mid), (1, mid))
            ]
        )

    def to_mid(t):
        first[t][0].wait_recv()
        for f in range(n_far):
            out_x[t][f] = (wide(ins[t][f, 1 - mid, core]) + wide(near[t][0, f])).astype(
                out_x[t].dtype
            )
        second.append(push(out_x[t], in_x[t], x_send.at[t], x_recv.at[t], {"col": x_peer}))
        first[t][1].wait_recv()
        for f in range(n_far):
            total[t][f] = wide(ins[t][f, mid, core]) + wide(near[t][1, f])

    def to_far(t):
        second[t].wait_recv()
        for f in range(n_far):
            total[t][f] = total[t][f] + wide(in_x[t][f])
            out_far[t][f] = total[t][f].astype(out_far[t].dtype)
        for d, f in enumerate(fars):
            third.append(
                push(
                    out_far[t].at[f], in_far[t].at[d],
                    far_send.at[t, d], far_recv.at[t, d], {"col": index(f, mid, core)},
                )
            )

    acts, count = (to_core, to_mid, to_far), [0, 0, 0]

    def advance(stage, end):
        while count[stage] < end:
            acts[stage](count[stage])
            count[stage] += 1

    for t in range(pieces):
        if t in flush:
            advance(1, t)
            advance(2, t)
        advance(0, t + 1)
        advance(1, t + 1 - LAGS[0])
        advance(2, t + 1 - sum(LAGS))
    advance(1, pieces)
    advance(2, pieces)
    for t in range(pieces):
        value = total[t][far]
        for d in range(n_far - 1):
            third[t * (n_far - 1) + d].wait_recv()
            value = value + wide(in_far[t][d])
        finish(t, value)
    for made in sends:
        made.wait_send()


def reduce_scratch(n_col, block, kind):
    n_far = n_col // 4
    dma = pltpu.SemaphoreType.DMA
    pieces = len(block)

    def buffers(lead, dtype=kind):
        return [pltpu.VMEM(lead + tuple(b), dtype) for b in block]

    return (
        buffers((2, n_far))
        + buffers((n_far,))
        + buffers((n_far,))
        + buffers((n_far,), jnp.float32)
        + buffers((n_far,))
        + buffers((n_far - 1,))
        + [
            dma((pieces, 2)), dma((pieces, 2)), dma((pieces,)), dma((pieces,)),
            dma((pieces, n_far - 1)), dma((pieces, n_far - 1)),
        ]
    )


def scatter_kernel(n_col, pieces, *refs):
    me, far, mid, core, index = place(n_col)
    n_far = n_col // 4
    fars = [lax.rem(far + d, n_far) for d in range(1, n_far)]
    greet(
        [index(far, mid, 1 - core), index(far, 1 - mid, core)]
        + [index(f, mid, core) for f in fars],
        [],
    )
    outs = refs[pieces : 2 * pieces]

    def finish(t, value):
        outs[t][...] = value.astype(outs[t].dtype)

    reduce_rows(n_col, pieces, refs[:pieces], refs[2 * pieces :], lambda t: None, finish)


def scatter(n_col, terms):
    pieces = len(terms)
    block, kind = [t.shape[-2:] for t in terms], terms[0].dtype
    return pl.pallas_call(
        functools.partial(scatter_kernel, n_col, pieces),
        out_shape=[jax.ShapeDtypeStruct(b, kind) for b in block],
        in_specs=[VMEM] * pieces,
        out_specs=[VMEM] * pieces,
        scratch_shapes=reduce_scratch(n_col, block, kind),
        compiler_params=pltpu.CompilerParams(collective_id=1, has_side_effects=True),
    )(*terms)


def fused_kernel(n_col, slab, occ, vir, screen, *refs):
    out_occ, out_vir = refs[:2]
    slabs, own_occ, own_vir, peer_occ, peer_vir, screens, occ_side, vir_side = refs[2:10]
    green, done, refs = refs[10], refs[11:15], refs[15:]
    cuts = cut_pieces(own_vir.shape[0], own_occ.shape[0])
    pieces = len(cuts)
    parts, refs = refs[:pieces], refs[pieces:]
    local_sem, load_sem, orb_send, orb_recv = refs[:4]
    spread_sems, reduce_refs = refs[4:8], refs[8:]
    n_far = n_col // 4
    me = lax.axis_index("col")
    other = 1 - lax.axis_index("orb")
    n_occ, columns = occ.shape
    n_vir = vir.shape[0]
    block, full = slabs.shape[2:]
    wide_vir = own_vir.shape[0]
    tile = 2 * 4 * block
    greet([lax.rem(me + d, n_col) for d in range(1, n_col)], [other])
    sends, push = sender()
    chunks = [(start, size) for kind, start, size in cuts if kind == 1]
    last = len(chunks) + 1
    push(slab.at[other], slabs.at[1, me], orb_send.at[last], spread_sems[1].at[1, me], {"orb": other})
    push(occ, peer_occ.at[pl.ds(0, n_occ)], orb_send.at[0], orb_recv.at[0], {"orb": other})

    def chunk_rows(c):
        start, size = chunks[c]
        return pl.ds(start, min(size, n_vir - start))

    for c in range(len(chunks)):
        push(vir.at[chunk_rows(c)], peer_vir.at[chunk_rows(c)], orb_send.at[1 + c],
             orb_recv.at[1 + c], {"orb": other})
    loads = []
    for n, (src, own, peer, rows) in enumerate(
        ((vir, own_vir, peer_vir, n_vir), (occ, own_occ, peer_occ, n_occ))
    ):
        load = pltpu.make_async_copy(src, own.at[pl.ds(0, rows)], load_sem.at[n])
        load.start()
        loads.append(load)
        short = own.shape[0] - rows
        if short:
            for ref in (own, peer):
                ref[pl.ds(rows, short)] = jnp.zeros((short, columns), ref.dtype)
    spread(n_col, push, last, slab, screen, slabs, screens, local_sem, orb_send, *spread_sems)
    for load in loads:
        load.wait()
    kinds = ((vir_side, own_vir), (vir_side, peer_vir), (occ_side, own_occ), (occ_side, peer_occ))

    def dot(a, b):
        return jnp.dot(a, b, preferred_element_type=jnp.float32)

    def each_tile(act):
        @pl.loop(0, n_far // 2)
        def _(i):
            act(i, pl.ds(pl.multiple_of(i * tile, tile), tile))

    def rows_of(k, i, lanes):
        return slabs[k, pl.ds(i * 8, 8), :, lanes].reshape((tile, -1))

    def each_cut(act):
        def rows_act(i, rows):
            for start in range(0, columns, 256):
                act(i, rows, pl.ds(start, 256))

        each_tile(rows_act)

    def shade(i, cut):
        return screens[pl.ds(i * 8, 8), :, cut].reshape((tile, -1)).astype(jnp.float32)

    def make_vir_side(i, rows, cut):
        lanes = slice(wide_vir, full)
        value = dot(rows_of(0, i, lanes), own_occ[:, cut])
        value = value + dot(rows_of(1, i, lanes), peer_occ[:, cut])
        vir_side[rows, cut] = (value * shade(i, cut)).astype(vir_side.dtype)

    def own_green(i, rows, cut):
        green[rows, cut] = dot(rows_of(0, i, slice(0, wide_vir)), own_vir[:, cut])

    def peer_green(c):
        start, size = chunks[c]

        def act(i, rows, cut):
            term = dot(rows_of(1, i, slice(start, start + size)), peer_vir[pl.ds(start, size), cut])
            green[rows, cut] = green[rows, cut] + term

        return act

    def make_occ_side(i, rows, cut):
        occ_side[rows, cut] = (green[rows, cut] * shade(i, cut)).astype(occ_side.dtype)

    def project(t):
        kind, start, size = cuts[t]
        side, orbs = kinds[kind]

        def act(i, rows):
            term = lax.dot_general(
                side[rows], orbs[pl.ds(start, size)], (((1,), (1,)), ((), ())),
                preferred_element_type=jnp.float32,
            )
            term = term.astype(parts[t].dtype)
            parts[t][pl.ds(i * 2, 2)] = term.reshape((2,) + parts[t].shape[1:])

        each_tile(act)

    landed(peer_occ.at[pl.ds(0, n_occ)], orb_send.at[0], orb_recv.at[0], {"orb": other})
    each_cut(make_vir_side)
    head = len(chunks)

    def ready(t):
        if t == head:
            each_cut(own_green)
        if head <= t < 2 * head:
            c = t - head
            landed(peer_vir.at[chunk_rows(c)], orb_send.at[1 + c], orb_recv.at[1 + c], {"orb": other})
            each_cut(peer_green(c))
        if t == 2 * head:
            each_cut(make_occ_side)
        project(t)

    def finish(t, value):
        kind, start, size = cuts[t]
        done[kind][:, pl.ds(start, size)] = value

    reduce_rows(
        n_col, pieces, parts, reduce_refs, ready, finish, (2 * head - 2, 2 * head - 1)
    )
    low = other == 1
    for out, own, peer, n in ((out_vir, done[0], done[1], n_vir), (out_occ, done[2], done[3], n_occ)):
        own, peer = own[:, :n], peer[:, :n]
        out[:, :n] = jnp.where(low, own, peer).astype(out.dtype)
        out[:, n:] = jnp.where(low, peer, own).astype(out.dtype)
    for copy in sends:
        copy.wait_send()


def cut_pieces(wide_vir, wide_occ):
    return [
        (kind, start, min(256, wide - start))
        for kind, wide in enumerate((wide_vir, wide_vir, wide_occ, wide_occ))
        for start in range(0, wide, 256)
    ]


def fused(n_col, slab, occ, vir, screen):
    block, full = slab.shape[1:]
    columns = occ.shape[1]
    kind = slab.dtype
    n_orb = slab.shape[0]
    wide_vir = -(-vir.shape[0] // 128) * 128
    wide_occ = full - wide_vir
    widths = [size for kind, start, size in cut_pieces(wide_vir, wide_occ)]
    rows = n_col * block
    chunks = len(range(0, wide_vir, 256))
    dma = pltpu.SemaphoreType.DMA
    return pl.pallas_call(
        functools.partial(fused_kernel, n_col),
        out_shape=[
            jax.ShapeDtypeStruct((block, n_orb * orbs.shape[0]), kind) for orbs in (occ, vir)
        ],
        in_specs=[ANY] * 4,
        out_specs=[VMEM] * 2,
        scratch_shapes=[
            pltpu.VMEM((2, n_col, block, full), kind),
            pltpu.VMEM((wide_occ, columns), kind),
            pltpu.VMEM((wide_vir, columns), kind),
            pltpu.VMEM((wide_occ, columns), kind),
            pltpu.VMEM((wide_vir, columns), kind),
            pltpu.VMEM(screen.shape, kind),
            pltpu.VMEM((rows, columns), kind),
            pltpu.VMEM((rows, columns), kind),
            pltpu.VMEM((rows, columns), jnp.float32),
        ]
        + [pltpu.VMEM((block, w), jnp.float32) for w in (wide_vir, wide_vir, wide_occ, wide_occ)]
        + [pltpu.VMEM((n_col // 4, 2, 2, block, w), kind) for w in widths]
        + [dma((2,)), dma((2,)), dma((chunks + 2,)), dma((chunks + 1,))]
        + spread_semaphores(n_col)
        + reduce_scratch(n_col, [(block, w) for w in widths], kind),
        compiler_params=pltpu.CompilerParams(collective_id=2, has_side_effects=True),
    )(slab, occ, vir, screen)


def local(slab_occ, slab_vir, orbitals_occ, orbitals_vir, occ_energy, vir_energy, screened):
    n_orb, n_col = lax.axis_size("orb"), lax.axis_size("col")
    part = lax.axis_index("orb")
    block = slab_occ.shape[0] // n_orb
    n_occ, columns = orbitals_occ.shape
    n_vir = orbitals_vir.shape[0]
    kind = slab_occ.dtype
    up = lambda n: -(-n // 128) * 128
    scaled_occ = (slab_occ.astype(jnp.float32) * jnp.exp(occ_energy)[None, :]).astype(kind)
    scaled_vir = (slab_vir.astype(jnp.float32) * jnp.exp(-vir_energy)[None, :]).astype(kind)
    start = up(n_vir)
    slab = jnp.concatenate(
        [
            jnp.pad(scaled_vir, ((0, 0), (0, start - n_vir))),
            jnp.pad(scaled_occ, ((0, 0), (0, up(n_occ) - n_occ))),
        ],
        axis=1,
    ).reshape((n_orb, block, start + up(n_occ)))
    mine = lax.dynamic_slice_in_dim(screened, part * block, block, 0)
    mine = mine.reshape((block, n_col, columns)).transpose((1, 0, 2))

    def order(own, peer, n):
        own, peer = own[:, :n], peer[:, :n]
        return jnp.where(
            part == 0, jnp.concatenate([own, peer], 1), jnp.concatenate([peer, own], 1)
        )

    if block % 16 == 0 and n_col % 8 == 0 and columns % 512 == 0:
        return tuple(fused(n_col, slab, orbitals_occ, orbitals_vir, mine))

    slabs, peer_occ, peer_vir, screens = gather(n_col, slab, orbitals_occ, orbitals_vir, mine)
    slabs = slabs.reshape((2, n_col * block, slab.shape[2]))
    own_slab, peer_slab = slabs[0], slabs[1]

    def dot(a, b):
        return jnp.dot(a, b, preferred_element_type=jnp.float32)

    green_vir = dot(own_slab[:, :n_vir], orbitals_vir) + dot(peer_slab[:, :n_vir], peer_vir)
    green_occ = dot(own_slab[:, start : start + n_occ], orbitals_occ) + dot(
        peer_slab[:, start : start + n_occ], peer_occ
    )
    screen = screens.reshape((n_col * block, columns)).astype(jnp.float32)
    occ_side = (green_vir * screen).astype(kind)
    vir_side = (green_occ * screen).astype(kind)
    dims = (((1,), (1,)), ((), ()))

    def project(side, orbitals):
        term = lax.dot_general(side, orbitals, dims, preferred_element_type=jnp.float32)
        return term.astype(kind).reshape((n_col // 4, 2, 2, block, orbitals.shape[0]))

    vir_own, vir_peer, occ_own, occ_peer = scatter(
        n_col,
        [
            project(vir_side, orbitals_vir),
            project(vir_side, peer_vir),
            project(occ_side, orbitals_occ),
            project(occ_side, peer_occ),
        ],
    )

    return order(occ_own, occ_peer, n_occ), order(vir_own, vir_peer, n_vir)


def solution(mesh):
    return jax.shard_map(
        local,
        mesh=mesh,
        in_specs=(
            P("col", "orb"),
            P("col", "orb"),
            P("orb", "col"),
            P("orb", "col"),
            P("orb"),
            P("orb"),
            P("col", None),
        ),
        out_specs=(P(("col", "orb"), None), P(("col", "orb"), None)),
        check_vma=False,
    )
```

profile of v0, /device:TPU:0, one launch (start us, length us, event | category | flops | bytes accessed | tf_op | source)
XLA Modules:
  0.0 96.2 jit_solution(781503439292249)
XLA Ops:
  0.6 0.0 copy-start
  0.7 1.6 %copy-done = bf16[64,16384]{1,0:T(8,128)(2,1)S(1)} copy-done((bf16[64,16384]{1,0:T(8,128)(2,1)S(1)}, bf16[64,16384]{1,0:T(8,128)(2,1)}, u32[]{:S(2)}) %copy-start) | copy-done | bytes 2097176
  2.2 0.0 copy-start.3
  2.2 0.0 copy-start.1
  2.2 0.0 copy-start.4
  2.2 0.0 copy-start.2
  2.2 0.1 constant_dynamic-slice_fusion
  2.3 1.1 %copy.12 = bf16[4,16,8,1024]{3,2,0,1:T(8,128)(2,1)} copy(bf16[4,16,8,1024]{3,2,1,0:T(8,128)(2,1)S(1)} %bitcast.8) | data formatting | bytes 2097152 | tf_op jit(solution)/shard_map/reshape | solution.py:480
  3.4 0.0 copy-done.3
  3.4 0.0 copy-done.1
  3.4 0.0 copy-done.4
  3.5 0.0 copy-done.2
  3.5 0.7 fusion.2
  4.2 89.1 %shard_map.86 = (bf16[32,400]{1,0:T(8,128)(2,1)}, bf16[32,2400]{1,0:T(8,128)(2,1)}) custom-call(bf16[2,32,1536]{2,1,0:T(8,128)(2,1)} %bitcast.10, bf16[200,1024]{1,0:T(8,128)(2,1)} %occ.1, bf16[1200,1024]{1,0:T(8,128)(2,1)} %vir.1, bf16[16,32,1024]{2,1,0:T(8,128)(2,1)} %bitcast.9), custom_call_target="tpu_custom_call" | custom-call | tf_op jit(solution)/shard_map/pallas_call | solution.py:434
  93.3 1.4 %copy.15 = bf16[32,400]{1,0:T(8,128)(2,1)} copy(bf16[32,400]{1,0:T(8,128)(2,1)} %get-tuple-element.4) | data formatting | bytes 51200
  94.6 1.6 %copy.16 = bf16[32,2400]{1,0:T(8,128)(2,1)} copy(bf16[32,2400]{1,0:T(8,128)(2,1)} %get-tuple-element.5) | data formatting | bytes 307200
  (4 shorter events, 0.1 us)
Async XLA Ops:
  0.6 1.6 %copy-start = (bf16[64,16384]{1,0:T(8,128)(2,1)S(1)}, bf16[64,16384]{1,0:T(8,128)(2,1)}, u32[]{:S(2)}) copy-start(bf16[64,16384]{1,0:T(8,128)(2,1)} %param.13) | copy-start | bytes 6291460
  2.2 1.2 %copy-start.3 = (f32[1200]{0:T(1024)S(1)}, f32[1200]{0:T(1024)}, u32[]{:S(2)}) copy-start(f32[1200]{0:T(1024)} %param.12) | copy-start | bytes 14404
  2.2 1.2 %copy-start.1 = (bf16[64,1200]{1,0:T(8,128)(2,1)S(1)}, bf16[64,1200]{1,0:T(8,128)(2,1)}, u32[]{:S(2)}) copy-start(bf16[64,1200]{1,0:T(8,128)(2,1)} %param.8) | copy-start | bytes 460804
  2.2 1.2 %copy-start.4 = (f32[200]{0:T(256)S(1)}, f32[200]{0:T(256)}, u32[]{:S(2)}) copy-start(f32[200]{0:T(256)} %param.11) | copy-start | bytes 2404
  2.2 1.2 %copy-start.2 = (bf16[64,200]{1,0:T(8,128)(2,1)S(1)}, bf16[64,200]{1,0:T(8,128)(2,1)}, u32[]{:S(2)}) copy-start(bf16[64,200]{1,0:T(8,128)(2,1)} %param.7) | copy-start | bytes 76804
where the time goes:
time: 96.5 us; the launch traced here: 96.2 us
  Pallas kernels  89.1 us (92%)
  local copies, waits for them, and re-layouts  5.71 us (6%)
    pallas_call x1, Pallas kernels, fused(): pl.pallas_call(functools.partial(fused_kernel, n_col), out_shape=[jax.Sha...  89.1 us
    unnamed x12, local copies, waits for them, and re-layouts  4.56 us

commit v1 on v0

--- a/solution.py
+++ b/solution.py
@@ -278,184 +278,400 @@
     )(*terms)
 
 
-def fused_kernel(n_col, slab, occ, vir, screen, *refs):
+def order(far, j):
+    if j == 0:
+        return far
+    if j == 1:
+        return far + 1 - 2 * lax.rem(far, 2)
+    return 2 - far // 2 if j == 2 else 3 - 3 * (far // 2)
+
+
+def fused_kernel(n_col, slab_occ, slab_vir, occ, vir, occ_energy, vir_energy, screen, *refs):
     out_occ, out_vir = refs[:2]
-    slabs, own_occ, own_vir, peer_occ, peer_vir, screens, occ_side, vir_side = refs[2:10]
-    green, done, refs = refs[10], refs[11:15], refs[15:]
-    cuts = cut_pieces(own_vir.shape[0], own_occ.shape[0])
-    pieces = len(cuts)
-    parts, refs = refs[:pieces], refs[pieces:]
-    local_sem, load_sem, orb_send, orb_recv = refs[:4]
-    spread_sems, reduce_refs = refs[4:8], refs[8:]
+    (raw_occ, raw_vir, e_occ, e_vir, sv, so, ov, od, screens, green, green_out, green_in, side,
+     part_vir, part_occ, near_vir, near_occ, out_x_vir, out_x_occ, in_x_vir, in_x_occ,
+     sum_vir, sum_occ, out_far_vir, out_far_occ, in_far_vir, in_far_occ,
+     end_out_vir, end_out_occ, end_in_vir, end_in_occ) = refs[2:33]
+    (load_sem, slab_send, slab_recv, swap_send, swap_recv, screen_send, screen_recv,
+     green_send, green_recv, side_send, side_recv, near_send, near_recv, x_send, x_recv,
+     far_send, far_recv, end_send, end_recv) = refs[33:]
     n_far = n_col // 4
-    me = lax.axis_index("col")
-    other = 1 - lax.axis_index("orb")
+    me, far, mid, core, index = place(n_col)
+    part = lax.axis_index("orb")
+    other = 1 - part
+    x_peer, core_peer = index(far, 1 - mid, core), index(far, mid, 1 - core)
+    diagonal = index(far, 1 - mid, 1 - core)
+    inner = lax.rem(far, 3) > 0
+    planes = [order(far, j) for j in range(n_far)]
+    n_occ = occ.shape[0]
+    n_vir = vir.shape[0]
+    half = ov.shape[2]
+    block = sv.shape[1]
+    rows = 4 * block
+    kind = sv.dtype
+    wide = lambda value: value.astype(jnp.float32)
+
+    def dot(a, b):
+        return jnp.dot(a, b, preferred_element_type=jnp.float32)
+
+    def dot_t(a, b):
+        return lax.dot_general(a, b, (((1,), (1,)), ((), ())), preferred_element_type=jnp.float32)
+
+    barrier = pltpu.get_barrier_semaphore()
+    for d in range(1, n_col):
+        pl.semaphore_signal(
+            barrier, inc=1, device_id={"col": lax.rem(me + d, n_col)}, device_id_type=MESH
+        )
+    pl.semaphore_signal(barrier, inc=1, device_id={"orb": other}, device_id_type=MESH)
+
+    def piece(p, k):
+        start = p * (2 * half) + k * half
+        return screen.at[:, pl.ds(pl.multiple_of(start, half), half)]
+
+    def columns_of(ref, k):
+        return ref.at[:, pl.ds(pl.multiple_of(k * half, half), half)]
+
+    loads = [
+        pltpu.make_async_copy(src, dst, load_sem.at[n])
+        for n, (src, dst) in enumerate(
+            (
+                (vir_energy, e_vir), (slab_vir, raw_vir), (occ_energy, e_occ), (slab_occ, raw_occ),
+                (columns_of(vir, other), ov.at[other, pl.ds(0, n_vir)]),
+                (columns_of(vir, part), ov.at[part, pl.ds(0, n_vir)]),
+                (columns_of(occ, part), od.at[part, pl.ds(0, n_occ)]),
+                (piece(me, part), screens.at[me]),
+            )
+        )
+    ]
+    for load in loads:
+        load.start()
+    for ref, n in ((ov, n_vir), (od, n_occ)):
+        short = ref.shape[1] - n
+        if short:
+            for k in range(2):
+                ref[k, pl.ds(n, short)] = jnp.zeros((short, half), kind)
+    for load in loads[:4]:
+        load.wait()
+    sv[me, :, :n_vir] = (wide(raw_vir[...]) * jnp.exp(-e_vir[...])).astype(kind)
+    if sv.shape[2] > n_vir:
+        sv[me, :, n_vir:] = jnp.zeros((block, sv.shape[2] - n_vir), kind)
+    so[me, part, :, :n_occ] = (wide(raw_occ[...]) * jnp.exp(e_occ[...])).astype(kind)
+    if so.shape[3] > n_occ:
+        so[me, part, :, n_occ:] = jnp.zeros((block, so.shape[3] - n_occ), kind)
+    pl.semaphore_wait(barrier, n_col)
+
+    sends = []
+
+    def push(src, dst, send, recv, device, only=None):
+        copy = pltpu.make_async_remote_copy(
+            src_ref=src, dst_ref=dst, send_sem=send, recv_sem=recv,
+            device_id=device, device_id_type=MESH,
+        )
+        if only is None:
+            copy.start()
+        else:
+            pl.when(only)(copy.start)
+        sends.append((only, copy))
+        return copy
+
+    slabs = (sv, so)
+    counter = [0]
+
+    def give(k, col, target, only=None):
+        push(slabs[k].at[col], slabs[k].at[col], slab_send.at[counter[0]], slab_recv.at[k, col],
+             {"col": target}, only)
+        counter[0] += 1
+
+    def arrived(k, col):
+        landed(slabs[k].at[col], swap_send.at[0], slab_recv.at[k, col], {"orb": other})
+
+    def give_own(k):
+        give(k, me, x_peer)
+        give(k, me, index(planes[1], mid, core))
+        give(k, me, index(3 - far, mid, core), inner)
+        give(k, me, core_peer)
+
+    def relay(k, j):
+        col = index(planes[j], mid, core)
+        arrived(k, col)
+        step = 3 - far if j == 1 else 3 * far - 3
+        give(k, col, index(step, mid, core), inner)
+        give(k, col, x_peer)
+        give(k, col, core_peer)
+
+    def cross(k, j):
+        col = index(planes[j], 1 - mid, core)
+        arrived(k, col)
+        give(k, col, core_peer)
+
+    def settle(k, j):
+        arrived(k, index(planes[j], mid, 1 - core))
+        arrived(k, index(planes[j], 1 - mid, 1 - core))
+
+    screen_count = [0]
+
+    def give_screen(target):
+        push(piece(target, part), screens.at[me], screen_send.at[screen_count[0]],
+             screen_recv.at[me], {"col": target})
+        screen_count[0] += 1
+
+    def give_screens(j):
+        for m, c in ((mid, core), (1 - mid, core), (mid, 1 - core), (1 - mid, 1 - core)):
+            give_screen(index(planes[j], m, c))
+
+    def screened(j):
+        for m, c in ((mid, core), (1 - mid, core), (mid, 1 - core), (1 - mid, 1 - core)):
+            if j == 0 and m is mid and c is core:
+                loads[7].wait()
+            else:
+                col = index(planes[j], m, c)
+                landed(screens.at[col], swap_send.at[0], screen_recv.at[col], {"orb": other})
+
+    def plane(j):
+        return pl.ds(planes[j] * 4, 4)
+
+    def shade(j, cut):
+        return wide(screens[plane(j), :, cut].reshape((rows, -1)))
+
+    cuts = [slice(start, start + 256) for start in range(0, half, 256)]
+    swaps = {}
+
+    def make_green(j):
+        slab = sv[plane(j)].reshape((rows, -1))
+        for cut in cuts:
+            green_out[j, :, cut] = dot(slab, ov[other, :, cut]).astype(kind)
+        swaps["green", j] = push(green_out.at[j], green_in.at[j], green_send.at[j],
+                                 green_recv.at[j], {"orb": other})
+        for cut in cuts:
+            green[j, :, cut] = dot(slab, ov[part, :, cut])
+
+    def make_side(j):
+        for cut in cuts:
+            value = dot(so[plane(j), 0].reshape((rows, -1)), od[0, :, cut])
+            value = value + dot(so[plane(j), 1].reshape((rows, -1)), od[1, :, cut])
+            side[j, part, :, cut] = (value * shade(j, cut)).astype(kind)
+        swaps["side", j] = push(side.at[j, part], side.at[j, part], side_send.at[j],
+                                side_recv.at[j], {"orb": other})
+
+    class Reduce:
+        def __init__(self, n, part, near, out_x, in_x, total, out_far, in_far, end_out, end_in):
+            self.n, self.part, self.near, self.out_x, self.in_x = n, part, near, out_x, in_x
+            self.total, self.out_far, self.in_far = total, out_far, in_far
+            self.end_out, self.end_in = end_out, end_in
+            self.first, self.second, self.third = {}, {}, {}
+
+        def to_core(self, j):
+            n = self.n
+            self.first[j] = [
+                push(self.part.at[j, m, 1 - core], self.near.at[j, slot],
+                     near_send.at[n, j, slot], near_recv.at[n, j, slot], {"col": core_peer})
+                for slot, m in ((0, 1 - mid), (1, mid))
+            ]
+
+        def to_mid(self, j):
+            n = self.n
+            self.first[j][0].wait_recv()
+            self.out_x[j] = (wide(self.part[j, 1 - mid, core]) + wide(self.near[j, 0])).astype(kind)
+            self.second[j] = push(self.out_x.at[j], self.in_x.at[j], x_send.at[n, j],
+                                  x_recv.at[n, j], {"col": x_peer})
+            self.first[j][1].wait_recv()
+            self.total[j] = wide(self.part[j, mid, core]) + wide(self.near[j, 1])
+
+        def to_far(self, j):
+            n = self.n
+            self.second[j].wait_recv()
+            value = self.total[j] + wide(self.in_x[j])
+            if j == 0:
+                self.total[0] = value
+            else:
+                self.out_far[j - 1] = value.astype(kind)
+                push(self.out_far.at[j - 1], self.in_far.at[far], far_send.at[n, j - 1],
+                     far_recv.at[n, far], {"col": index(planes[j], mid, core)})
+
+        def gather(self):
+            n = self.n
+            value = self.total[0]
+            for j in range(1, n_far):
+                source = planes[j]
+                landed(self.in_far.at[source], swap_send.at[0], far_recv.at[n, source], {"orb": other})
+                value = value + wide(self.in_far[source])
+            self.total[0] = value
+            lines = block // 2
+            mine = pl.ds(pl.multiple_of(part * lines, lines), lines)
+            theirs = pl.ds(pl.multiple_of(other * lines, lines), lines)
+            self.end_out[...] = self.total[0, theirs].astype(kind)
+            self.last = push(self.end_out, self.end_in, end_send.at[n], end_recv.at[n], {"orb": other})
+            self.mine = mine
+
+        def end(self):
+            self.last.wait_recv()
+            return self.total[0, self.mine], wide(self.end_in[...])
+
+    of_vir = Reduce(0, part_vir, near_vir, out_x_vir, in_x_vir, sum_vir, out_far_vir, in_far_vir,
+                    end_out_vir, end_in_vir)
+    of_occ = Reduce(1, part_occ, near_occ, out_x_occ, in_x_occ, sum_occ, out_far_occ, in_far_occ,
+                    end_out_occ, end_in_occ)
+
+    def project_vir(j):
+        swaps["side", j].wait_recv()
+        width = part_vir.shape[-1]
+        for start in range(0, width, 256):
+            cut = slice(start, min(start + 256, width))
+            term = dot_t(side[j, 0], ov[0, cut]) + dot_t(side[j, 1], ov[1, cut])
+            part_vir[j, :, :, :, cut] = term.astype(kind).reshape((2, 2, block, -1))
+        of_vir.to_core(j)
+
+    def project_occ(j):
+        swaps["green", j].wait_recv()
+        value = (green[j] + wide(green_in[j])) * shade(j, slice(0, half))
+        value = value.astype(kind)
+        wide_occ = od.shape[1]
+        for k in range(2):
+            term = dot_t(value, od[k]).astype(kind)
+            part_occ[j, :, :, :, slice(k * wide_occ, (k + 1) * wide_occ)] = term.reshape(
+                (2, 2, block, -1)
+            )
+        of_occ.to_core(j)
+
+    push(so.at[me, part], so.at[me, part], swap_send.at[0], swap_recv.at[0], {"orb": other})
+    swap = push(columns_of(occ, other), od.at[part, pl.ds(0, n_occ)], swap_send.at[1],
+                swap_recv.at[1], {"orb": other})
+    give_own(0)
+    for target in (x_peer, core_peer, diagonal):
+        give_screen(target)
+    give_screens(1)
+    landed(so.at[me, other], swap_send.at[0], swap_recv.at[0], {"orb": other})
+    give_own(1)
+    for load in loads[4:7]:
+        load.wait()
+    cross(0, 0)
+    relay(0, 1)
+    settle(0, 0)
+    make_green(0)
+    cross(1, 0)
+    relay(1, 1)
+    give_screens(2)
+    settle(1, 0)
+    screened(0)
+    swap.wait_recv()
+    make_side(0)
+    relay(0, 2)
+    relay(1, 2)
+    give_screens(3)
+    cross(0, 1)
+    settle(0, 1)
+    make_green(1)
+    cross(1, 1)
+    settle(1, 1)
+    screened(1)
+    make_side(1)
+    relay(0, 3)
+    relay(1, 3)
+    cross(0, 2)
+    cross(1, 2)
+    settle(0, 2)
+    make_green(2)
+    project_vir(0)
+    project_occ(0)
+    settle(1, 2)
+    of_vir.to_mid(0)
+    screened(2)
+    make_side(2)
+    of_occ.to_mid(0)
+    cross(0, 3)
+    cross(1, 3)
+    settle(0, 3)
+    settle(1, 3)
+    screened(3)
+    make_side(3)
+    make_green(3)
+    of_vir.to_far(0)
+    of_occ.to_far(0)
+    for j in range(1, n_far):
+        vir_first = j < n_far - 1
+        acts = [(project_vir, of_vir), (project_occ, of_occ)]
+        for act, _ in acts:
+            act(j)
+        for _, reduce in acts:
+            if j > 1:
+                reduce.to_far(j - 1)
+            reduce.to_mid(j)
+    for reduce in (of_vir, of_occ):
+        reduce.to_far(n_far - 1)
+    of_vir.gather()
+    of_occ.gather()
+    low = part == 0
+    own, peer = of_vir.end()
+    own, peer = own[:, :n_vir], peer[:, :n_vir]
+    out_vir[:, :n_vir] = jnp.where(low, own, peer).astype(kind)
+    out_vir[:, n_vir:] = jnp.where(low, peer, own).astype(kind)
+    own, peer = of_occ.end()
+    value = own + peer
+    wide_occ = od.shape[1]
+    out_occ[:, :n_occ] = value[:, :n_occ].astype(kind)
+    out_occ[:, n_occ:] = value[:, wide_occ : wide_occ + n_occ].astype(kind)
+    for only, copy in sends:
+        if only is None:
+            copy.wait_send()
+        else:
+            pl.when(only)(copy.wait_send)
+
+
+def fused(n_col, slab_occ, slab_vir, occ, vir, occ_energy, vir_energy, screen):
+    up = lambda n: -(-n // 128) * 128
+    block = slab_occ.shape[0]
     n_occ, columns = occ.shape
     n_vir = vir.shape[0]
-    block, full = slabs.shape[2:]
-    wide_vir = own_vir.shape[0]
-    tile = 2 * 4 * block
-    greet([lax.rem(me + d, n_col) for d in range(1, n_col)], [other])
-    sends, push = sender()
-    chunks = [(start, size) for kind, start, size in cuts if kind == 1]
-    last = len(chunks) + 1
-    push(slab.at[other], slabs.at[1, me], orb_send.at[last], spread_sems[1].at[1, me], {"orb": other})
-    push(occ, peer_occ.at[pl.ds(0, n_occ)], orb_send.at[0], orb_recv.at[0], {"orb": other})
-
-    def chunk_rows(c):
-        start, size = chunks[c]
-        return pl.ds(start, min(size, n_vir - start))
-
-    for c in range(len(chunks)):
-        push(vir.at[chunk_rows(c)], peer_vir.at[chunk_rows(c)], orb_send.at[1 + c],
-             orb_recv.at[1 + c], {"orb": other})
-    loads = []
-    for n, (src, own, peer, rows) in enumerate(
-        ((vir, own_vir, peer_vir, n_vir), (occ, own_occ, peer_occ, n_occ))
-    ):
-        load = pltpu.make_async_copy(src, own.at[pl.ds(0, rows)], load_sem.at[n])
-        load.start()
-        loads.append(load)
-        short = own.shape[0] - rows
-        if short:
-            for ref in (own, peer):
-                ref[pl.ds(rows, short)] = jnp.zeros((short, columns), ref.dtype)
-    spread(n_col, push, last, slab, screen, slabs, screens, local_sem, orb_send, *spread_sems)
-    for load in loads:
-        load.wait()
-    kinds = ((vir_side, own_vir), (vir_side, peer_vir), (occ_side, own_occ), (occ_side, peer_occ))
-
-    def dot(a, b):
-        return jnp.dot(a, b, preferred_element_type=jnp.float32)
-
-    def each_tile(act):
-        @pl.loop(0, n_far // 2)
-        def _(i):
-            act(i, pl.ds(pl.multiple_of(i * tile, tile), tile))
-
-    def rows_of(k, i, lanes):
-        return slabs[k, pl.ds(i * 8, 8), :, lanes].reshape((tile, -1))
-
-    def each_cut(act):
-        def rows_act(i, rows):
-            for start in range(0, columns, 256):
-                act(i, rows, pl.ds(start, 256))
-
-        each_tile(rows_act)
-
-    def shade(i, cut):
-        return screens[pl.ds(i * 8, 8), :, cut].reshape((tile, -1)).astype(jnp.float32)
-
-    def make_vir_side(i, rows, cut):
-        lanes = slice(wide_vir, full)
-        value = dot(rows_of(0, i, lanes), own_occ[:, cut])
-        value = value + dot(rows_of(1, i, lanes), peer_occ[:, cut])
-        vir_side[rows, cut] = (value * shade(i, cut)).astype(vir_side.dtype)
-
-    def own_green(i, rows, cut):
-        green[rows, cut] = dot(rows_of(0, i, slice(0, wide_vir)), own_vir[:, cut])
-
-    def peer_green(c):
-        start, size = chunks[c]
-
-        def act(i, rows, cut):
-            term = dot(rows_of(1, i, slice(start, start + size)), peer_vir[pl.ds(start, size), cut])
-            green[rows, cut] = green[rows, cut] + term
-
-        return act
-
-    def make_occ_side(i, rows, cut):
-        occ_side[rows, cut] = (green[rows, cut] * shade(i, cut)).astype(occ_side.dtype)
-
-    def project(t):
-        kind, start, size = cuts[t]
-        side, orbs = kinds[kind]
-
-        def act(i, rows):
-            term = lax.dot_general(
-                side[rows], orbs[pl.ds(start, size)], (((1,), (1,)), ((), ())),
-                preferred_element_type=jnp.float32,
-            )
-            term = term.astype(parts[t].dtype)
-            parts[t][pl.ds(i * 2, 2)] = term.reshape((2,) + parts[t].shape[1:])
-
-        each_tile(act)
-
-    landed(peer_occ.at[pl.ds(0, n_occ)], orb_send.at[0], orb_recv.at[0], {"orb": other})
-    each_cut(make_vir_side)
-    head = len(chunks)
-
-    def ready(t):
-        if t == head:
-            each_cut(own_green)
-        if head <= t < 2 * head:
-            c = t - head
-            landed(peer_vir.at[chunk_rows(c)], orb_send.at[1 + c], orb_recv.at[1 + c], {"orb": other})
-            each_cut(peer_green(c))
-        if t == 2 * head:
-            each_cut(make_occ_side)
-        project(t)
-
-    def finish(t, value):
-        kind, start, size = cuts[t]
-        done[kind][:, pl.ds(start, size)] = value
-
-    reduce_rows(
-        n_col, pieces, parts, reduce_refs, ready, finish, (2 * head - 2, 2 * head - 1)
-    )
-    low = other == 1
-    for out, own, peer, n in ((out_vir, done[0], done[1], n_vir), (out_occ, done[2], done[3], n_occ)):
-        own, peer = own[:, :n], peer[:, :n]
-        out[:, :n] = jnp.where(low, own, peer).astype(out.dtype)
-        out[:, n:] = jnp.where(low, peer, own).astype(out.dtype)
-    for copy in sends:
-        copy.wait_send()
-
-
-def cut_pieces(wide_vir, wide_occ):
-    return [
-        (kind, start, min(256, wide - start))
-        for kind, wide in enumerate((wide_vir, wide_vir, wide_occ, wide_occ))
-        for start in range(0, wide, 256)
-    ]
-
-
-def fused(n_col, slab, occ, vir, screen):
-    block, full = slab.shape[1:]
-    columns = occ.shape[1]
-    kind = slab.dtype
-    n_orb = slab.shape[0]
-    wide_vir = -(-vir.shape[0] // 128) * 128
-    wide_occ = full - wide_vir
-    widths = [size for kind, start, size in cut_pieces(wide_vir, wide_occ)]
-    rows = n_col * block
-    chunks = len(range(0, wide_vir, 256))
+    kind, f32 = slab_occ.dtype, jnp.float32
+    half = columns // 2
+    wide_occ, wide_vir = up(n_occ), up(n_vir)
+    n_far = n_col // 4
+    rows = 4 * block
+    both = 2 * wide_occ
     dma = pltpu.SemaphoreType.DMA
+
+    def pair(lead, lines, dtype=kind):
+        return [pltpu.VMEM(lead + (lines, w), dtype) for w in (wide_vir, both)]
+
     return pl.pallas_call(
         functools.partial(fused_kernel, n_col),
         out_shape=[
-            jax.ShapeDtypeStruct((block, n_orb * orbs.shape[0]), kind) for orbs in (occ, vir)
+            jax.ShapeDtypeStruct((block // 2, 2 * n), kind) for n in (n_occ, n_vir)
         ],
-        in_specs=[ANY] * 4,
+        in_specs=[ANY] * 7,
         out_specs=[VMEM] * 2,
         scratch_shapes=[
-            pltpu.VMEM((2, n_col, block, full), kind),
-            pltpu.VMEM((wide_occ, columns), kind),
-            pltpu.VMEM((wide_vir, columns), kind),
-            pltpu.VMEM((wide_occ, columns), kind),
-            pltpu.VMEM((wide_vir, columns), kind),
-            pltpu.VMEM(screen.shape, kind),
-            pltpu.VMEM((rows, columns), kind),
-            pltpu.VMEM((rows, columns), kind),
-            pltpu.VMEM((rows, columns), jnp.float32),
+            pltpu.VMEM(slab_occ.shape, kind),
+            pltpu.VMEM(slab_vir.shape, kind),
+            pltpu.VMEM(occ_energy.shape, f32),
+            pltpu.VMEM(vir_energy.shape, f32),
+            pltpu.VMEM((n_col, block, wide_vir), kind),
+            pltpu.VMEM((n_col, 2, block, wide_occ), kind),
+            pltpu.VMEM((2, wide_vir, half), kind),
+            pltpu.VMEM((2, wide_occ, half), kind),
+            pltpu.VMEM((n_col, block, half), kind),
+            pltpu.VMEM((n_far, rows, half), f32),
+            pltpu.VMEM((n_far, rows, half), kind),
+            pltpu.VMEM((n_far, rows, half), kind),
+            pltpu.VMEM((n_far, 2, rows, half), kind),
         ]
-        + [pltpu.VMEM((block, w), jnp.float32) for w in (wide_vir, wide_vir, wide_occ, wide_occ)]
-        + [pltpu.VMEM((n_col // 4, 2, 2, block, w), kind) for w in widths]
-        + [dma((2,)), dma((2,)), dma((chunks + 2,)), dma((chunks + 1,))]
-        + spread_semaphores(n_col)
-        + reduce_scratch(n_col, [(block, w) for w in widths], kind),
+        + pair((n_far, 2, 2), block)
+        + pair((n_far, 2), block)
+        + pair((n_far,), block)
+        + pair((n_far,), block)
+        + pair((n_far,), block, f32)
+        + pair((n_far - 1,), block)
+        + pair((n_far,), block)
+        + pair((), block // 2)
+        + pair((), block // 2)
+        + [
+            dma((8,)), dma((34,)), dma((2, n_col)), dma((2,)), dma((2,)), dma((n_col,)), dma((n_col,)),
+            dma((n_far,)), dma((n_far,)), dma((n_far,)), dma((n_far,)),
+            dma((2, n_far, 2)), dma((2, n_far, 2)), dma((2, n_far)), dma((2, n_far)),
+            dma((2, n_far - 1)), dma((2, n_far)), dma((2,)), dma((2,)),
+        ],
         compiler_params=pltpu.CompilerParams(collective_id=2, has_side_effects=True),
-    )(slab, occ, vir, screen)
+    )(slab_occ, slab_vir, occ, vir, occ_energy, vir_energy, screen)
 
 
 def local(slab_occ, slab_vir, orbitals_occ, orbitals_vir, occ_energy, vir_energy, screened):
@@ -465,6 +681,13 @@
     n_occ, columns = orbitals_occ.shape
     n_vir = orbitals_vir.shape[0]
     kind = slab_occ.dtype
+    if n_col == 16 and n_orb == 2 and block % 16 == 0 and columns % 512 == 0:
+        return tuple(
+            fused(
+                n_col, slab_occ, slab_vir, orbitals_occ, orbitals_vir,
+                occ_energy[None, :], vir_energy[None, :], screened,
+            )
+        )
     up = lambda n: -(-n // 128) * 128
     scaled_occ = (slab_occ.astype(jnp.float32) * jnp.exp(occ_energy)[None, :]).astype(kind)
     scaled_vir = (slab_vir.astype(jnp.float32) * jnp.exp(-vir_energy)[None, :]).astype(kind)
@@ -484,9 +707,6 @@
         return jnp.where(
             part == 0, jnp.concatenate([own, peer], 1), jnp.concatenate([peer, own], 1)
         )
-
-    if block % 16 == 0 and n_col % 8 == 0 and columns % 512 == 0:
-        return tuple(fused(n_col, slab, orbitals_occ, orbitals_vir, mine))
 
     slabs, peer_occ, peer_vir, screens = gather(n_col, slab, orbitals_occ, orbitals_vir, mine)
     slabs = slabs.reshape((2, n_col * block, slab.shape[2]))

time: 96.5 us -> 93.8 us (0.972)
  local copies, waits for them, and re-layouts: 5.71 us -> 4.26 us
    unnamed x12 -> x2, local copies, waits for them, and re-layouts: 4.56 us -> 2.96 us
    broadcast_in_dim x0 -> x1, local copies, waits for them, and re-layouts: none -> 1.29 us  [local(): vir_energy[None, :]]
    reshape x1 -> x0, local copies, waits for them, and re-layouts: 1.07 us -> none  [local(): mine = mine.reshape((block, n_col, columns)).transpose((1, 0, 2))]
where the time goes in v1:
time: 93.8 us; the launch traced here: 93.6 us
  Pallas kernels  88.7 us (95%)
  local copies, waits for them, and re-layouts  4.26 us (5%)
    pallas_call x1, Pallas kernels, fused(): pl.pallas_call(functools.partial(fused_kernel, n_col), out_shape=[jax.Sha...  88.7 us
    unnamed x2, local copies, waits for them, and re-layouts  2.96 us

profile of v1, /device:TPU:0, one launch (start us, length us, event | category | flops | bytes accessed | tf_op | source)
XLA Modules:
  0.0 93.6 jit_solution(16290870807835658737)
XLA Ops:
  0.6 1.3 %broadcast_in_dim.7.vir_energy = f32[1,1200]{1,0:T(1,128)} reshape(f32[1200]{0:T(1024)} %param.12) | data formatting | bytes 9600 | tf_op jit(solution)/shard_map/broadcast_in_dim | solution.py:688
  1.9 88.7 %shard_map.86 = (bf16[32,400]{1,0:T(8,128)(2,1)}, bf16[32,2400]{1,0:T(8,128)(2,1)}) custom-call(bf16[64,200]{1,0:T(8,128)(2,1)} %slab_occ.1, bf16[64,1200]{1,0:T(8,128)(2,1)} %slab_vir.1, bf16[200,1024]{1,0:T(8,128)(2,1)} %occ.1, bf16[1200,1024]{1,0:T(8,128)(2,1)} %vir.1, f32[1,200]{1,0:T(1,128)} %bitcast.1, f32[1,1200]{1,0:T(1,128)} %broadcast_in_dim.7.vir_energy, ...), custom_call_target="tpu_custom_call" | custom-call | tf_op jit(solution)/shard_map/pallas_call | solution.py:636
  90.6 1.4 %copy.11 = bf16[32,400]{1,0:T(8,128)(2,1)} copy(bf16[32,400]{1,0:T(8,128)(2,1)} %get-tuple-element.4) | data formatting | bytes 51200
  92.0 1.6 %copy.12 = bf16[32,2400]{1,0:T(8,128)(2,1)} copy(bf16[32,2400]{1,0:T(8,128)(2,1)} %get-tuple-element.5) | data formatting | bytes 307200

commit v2 on v1

--- a/solution.py
+++ b/solution.py
@@ -283,7 +283,7 @@
         return far
     if j == 1:
         return far + 1 - 2 * lax.rem(far, 2)
-    return 2 - far // 2 if j == 2 else 3 - 3 * (far // 2)
+    return lax.rem(far + 2, 4) if j == 2 else 3 - far
 
 
 def fused_kernel(n_col, slab_occ, slab_vir, occ, vir, occ_energy, vir_energy, screen, *refs):
@@ -300,8 +300,10 @@
     part = lax.axis_index("orb")
     other = 1 - part
     x_peer, core_peer = index(far, 1 - mid, core), index(far, mid, 1 - core)
-    diagonal = index(far, 1 - mid, 1 - core)
+    other_mid = 1 - mid
+    diagonal = index(far, other_mid, 1 - core)
     inner = lax.rem(far, 3) > 0
+    outer = lax.rem(far, 3) == 0
     planes = [order(far, j) for j in range(n_far)]
     n_occ = occ.shape[0]
     n_vir = vir.shape[0]
@@ -352,10 +354,10 @@
                 ref[k, pl.ds(n, short)] = jnp.zeros((short, half), kind)
     for load in loads[:4]:
         load.wait()
-    sv[me, :, :n_vir] = (wide(raw_vir[...]) * jnp.exp(-e_vir[...])).astype(kind)
+    sv[me, :, :n_vir] = (wide(raw_vir[...]) * jnp.exp(-e_vir[...])[None, :]).astype(kind)
     if sv.shape[2] > n_vir:
         sv[me, :, n_vir:] = jnp.zeros((block, sv.shape[2] - n_vir), kind)
-    so[me, part, :, :n_occ] = (wide(raw_occ[...]) * jnp.exp(e_occ[...])).astype(kind)
+    so[me, part, :, :n_occ] = (wide(raw_occ[...]) * jnp.exp(e_occ[...])[None, :]).astype(kind)
     if so.shape[3] > n_occ:
         so[me, part, :, n_occ:] = jnp.zeros((block, so.shape[3] - n_occ), kind)
     pl.semaphore_wait(barrier, n_col)
@@ -382,22 +384,26 @@
              {"col": target}, only)
         counter[0] += 1
 
-    def arrived(k, col):
-        landed(slabs[k].at[col], swap_send.at[0], slab_recv.at[k, col], {"orb": other})
+    def arrived(k, col, only=None):
+        def act():
+            landed(slabs[k].at[col], swap_send.at[0], slab_recv.at[k, col], {"orb": other})
+
+        act() if only is None else pl.when(only)(act)
 
     def give_own(k):
         give(k, me, x_peer)
         give(k, me, index(planes[1], mid, core))
-        give(k, me, index(3 - far, mid, core), inner)
+        give(k, me, index(planes[3], mid, core), inner)
         give(k, me, core_peer)
 
-    def relay(k, j):
+    def relay(k, j, only=None):
         col = index(planes[j], mid, core)
-        arrived(k, col)
-        step = 3 - far if j == 1 else 3 * far - 3
-        give(k, col, index(step, mid, core), inner)
-        give(k, col, x_peer)
-        give(k, col, core_peer)
+        arrived(k, col, only)
+        step = planes[3 if j == 1 else 1]
+        if only is not outer:
+            give(k, col, index(step, mid, core), inner)
+        give(k, col, x_peer, only)
+        give(k, col, core_peer, only)
 
     def cross(k, j):
         col = index(planes[j], 1 - mid, core)
@@ -436,14 +442,19 @@
     cuts = [slice(start, start + 256) for start in range(0, half, 256)]
     swaps = {}
 
-    def make_green(j):
-        slab = sv[plane(j)].reshape((rows, -1))
+    def chip(m):
+        return pl.ds(planes[0] * 4 + 2 * m, 2), pl.ds(pl.multiple_of(m * (2 * block), 2 * block), 2 * block)
+
+    def make_green(j, m=None):
+        owners, lines = (plane(j), pl.ds(0, rows)) if m is None else chip(m)
+        slot = j if m is not other_mid else n_far
+        slab = sv[owners].reshape((-1, sv.shape[2]))
         for cut in cuts:
-            green_out[j, :, cut] = dot(slab, ov[other, :, cut]).astype(kind)
-        swaps["green", j] = push(green_out.at[j], green_in.at[j], green_send.at[j],
-                                 green_recv.at[j], {"orb": other})
+            green_out[j, lines, cut] = dot(slab, ov[other, :, cut]).astype(kind)
+        swaps["green", slot] = push(green_out.at[j, lines], green_in.at[j, lines], green_send.at[slot],
+                                    green_recv.at[slot], {"orb": other})
         for cut in cuts:
-            green[j, :, cut] = dot(slab, ov[part, :, cut])
+            green[j, lines, cut] = dot(slab, ov[part, :, cut])
 
     def make_side(j):
         for cut in cuts:
@@ -460,21 +471,22 @@
             self.end_out, self.end_in = end_out, end_in
             self.first, self.second, self.third = {}, {}, {}
 
-        def to_core(self, j):
+        def to_core(self, j, slots=(0, 1)):
             n = self.n
-            self.first[j] = [
-                push(self.part.at[j, m, 1 - core], self.near.at[j, slot],
-                     near_send.at[n, j, slot], near_recv.at[n, j, slot], {"col": core_peer})
-                for slot, m in ((0, 1 - mid), (1, mid))
-            ]
+            for slot in slots:
+                m = (other_mid, mid)[slot]
+                self.first[j, slot] = push(
+                    self.part.at[j, m, 1 - core], self.near.at[j, slot],
+                    near_send.at[n, j, slot], near_recv.at[n, j, slot], {"col": core_peer},
+                )
 
         def to_mid(self, j):
             n = self.n
-            self.first[j][0].wait_recv()
+            self.first[j, 0].wait_recv()
             self.out_x[j] = (wide(self.part[j, 1 - mid, core]) + wide(self.near[j, 0])).astype(kind)
             self.second[j] = push(self.out_x.at[j], self.in_x.at[j], x_send.at[n, j],
                                   x_recv.at[n, j], {"col": x_peer})
-            self.first[j][1].wait_recv()
+            self.first[j, 1].wait_recv()
             self.total[j] = wide(self.part[j, mid, core]) + wide(self.near[j, 1])
 
         def to_far(self, j):
@@ -521,90 +533,109 @@
             part_vir[j, :, :, :, cut] = term.astype(kind).reshape((2, 2, block, -1))
         of_vir.to_core(j)
 
-    def project_occ(j):
-        swaps["green", j].wait_recv()
-        value = (green[j] + wide(green_in[j])) * shade(j, slice(0, half))
+    def project_occ(j, m=None):
+        slot = j if m is not other_mid else n_far
+        swaps["green", slot].wait_recv()
+        owners, lines = (plane(j), pl.ds(0, rows)) if m is None else chip(m)
+        shades = wide(screens[owners].reshape((-1, half)))
+        value = (green[j, lines] + wide(green_in[j, lines])) * shades
         value = value.astype(kind)
         wide_occ = od.shape[1]
         for k in range(2):
-            term = dot_t(value, od[k]).astype(kind)
-            part_occ[j, :, :, :, slice(k * wide_occ, (k + 1) * wide_occ)] = term.reshape(
-                (2, 2, block, -1)
-            )
-        of_occ.to_core(j)
+            term = dot_t(value, od[k]).astype(kind).reshape((-1, 2, block, wide_occ))
+            cut = slice(k * wide_occ, (k + 1) * wide_occ)
+            if m is None:
+                part_occ[j, :, :, :, cut] = term
+            else:
+                part_occ[j, m, :, :, cut] = term[0]
+        of_occ.to_core(j, (0, 1) if m is None else (0,) if m is other_mid else (1,))
 
     push(so.at[me, part], so.at[me, part], swap_send.at[0], swap_recv.at[0], {"orb": other})
     swap = push(columns_of(occ, other), od.at[part, pl.ds(0, n_occ)], swap_send.at[1],
                 swap_recv.at[1], {"orb": other})
     give_own(0)
+    for load in loads[4:7]:
+        load.wait()
+    arrived(0, core_peer)
+    make_green(0, mid)
+    landed(so.at[me, other], swap_send.at[0], swap_recv.at[0], {"orb": other})
+    give_own(1)
     for target in (x_peer, core_peer, diagonal):
         give_screen(target)
     give_screens(1)
-    landed(so.at[me, other], swap_send.at[0], swap_recv.at[0], {"orb": other})
-    give_own(1)
-    for load in loads[4:7]:
-        load.wait()
-    cross(0, 0)
-    relay(0, 1)
-    settle(0, 0)
-    make_green(0)
     cross(1, 0)
     relay(1, 1)
+    relay(1, 3, inner)
+    relay(0, 1)
     give_screens(2)
     settle(1, 0)
     screened(0)
     swap.wait_recv()
     make_side(0)
-    relay(0, 2)
-    relay(1, 2)
+    cross(0, 0)
+    relay(1, 2, inner)
     give_screens(3)
-    cross(0, 1)
-    settle(0, 1)
-    make_green(1)
+    relay(0, 3, inner)
     cross(1, 1)
     settle(1, 1)
     screened(1)
     make_side(1)
-    relay(0, 3)
-    relay(1, 3)
-    cross(0, 2)
+    relay(1, 2, outer)
+    cross(0, 1)
+    settle(0, 1)
+    make_green(1)
+    project_vir(0)
+    relay(1, 3, outer)
     cross(1, 2)
-    settle(0, 2)
-    make_green(2)
-    project_vir(0)
-    project_occ(0)
     settle(1, 2)
     of_vir.to_mid(0)
+    relay(0, 2, inner)
     screened(2)
     make_side(2)
-    of_occ.to_mid(0)
-    cross(0, 3)
     cross(1, 3)
-    settle(0, 3)
+    relay(0, 2, outer)
+    project_vir(1)
+    of_vir.to_far(0)
+    of_vir.to_mid(1)
     settle(1, 3)
     screened(3)
     make_side(3)
+    cross(0, 2)
+    settle(0, 2)
+    make_green(2)
+    relay(0, 3, outer)
+    project_vir(2)
+    of_vir.to_far(1)
+    of_vir.to_mid(2)
+    cross(0, 3)
+    settle(0, 3)
     make_green(3)
-    of_vir.to_far(0)
-    of_occ.to_far(0)
-    for j in range(1, n_far):
-        vir_first = j < n_far - 1
-        acts = [(project_vir, of_vir), (project_occ, of_occ)]
-        for act, _ in acts:
-            act(j)
-        for _, reduce in acts:
-            if j > 1:
-                reduce.to_far(j - 1)
-            reduce.to_mid(j)
-    for reduce in (of_vir, of_occ):
-        reduce.to_far(n_far - 1)
+    arrived(0, diagonal)
+    make_green(0, other_mid)
+    project_occ(0, mid)
+    project_occ(1)
+    of_occ.to_mid(1)
+    project_vir(3)
+    of_vir.to_far(2)
+    of_occ.to_far(1)
+    of_vir.to_mid(3)
+    project_occ(2)
+    of_occ.to_mid(2)
+    of_vir.to_far(3)
+    project_occ(3)
+    of_occ.to_far(2)
+    of_occ.to_mid(3)
     of_vir.gather()
-    of_occ.gather()
+    project_occ(0, other_mid)
+    of_occ.to_mid(0)
+    of_occ.to_far(3)
     low = part == 0
     own, peer = of_vir.end()
     own, peer = own[:, :n_vir], peer[:, :n_vir]
     out_vir[:, :n_vir] = jnp.where(low, own, peer).astype(kind)
     out_vir[:, n_vir:] = jnp.where(low, peer, own).astype(kind)
+    of_occ.to_far(0)
+    of_occ.gather()
     own, peer = of_occ.end()
     value = own + peer
     wide_occ = od.shape[1]
@@ -665,8 +696,8 @@
         + pair((), block // 2)
         + pair((), block // 2)
         + [
-            dma((8,)), dma((34,)), dma((2, n_col)), dma((2,)), dma((2,)), dma((n_col,)), dma((n_col,)),
-            dma((n_far,)), dma((n_far,)), dma((n_far,)), dma((n_far,)),
+            dma((8,)), dma((42,)), dma((2, n_col)), dma((2,)), dma((2,)), dma((n_col,)), dma((n_col,)),
+            dma((n_far + 1,)), dma((n_far + 1,)), dma((n_far,)), dma((n_far,)),
             dma((2, n_far, 2)), dma((2, n_far, 2)), dma((2, n_far)), dma((2, n_far)),
             dma((2, n_far - 1)), dma((2, n_far)), dma((2,)), dma((2,)),
         ],
@@ -685,7 +716,7 @@
         return tuple(
             fused(
                 n_col, slab_occ, slab_vir, orbitals_occ, orbitals_vir,
-                occ_energy[None, :], vir_energy[None, :], screened,
+                occ_energy, vir_energy, screened,
             )
         )
     up = lambda n: -(-n // 128) * 128

time: 93.8 us -> 85 us (0.906)
  Pallas kernels: 88.7 us -> 80.9 us
  local copies, waits for them, and re-layouts: 4.26 us -> 2.96 us
    pallas_call x1, Pallas kernels: 88.7 us -> 80.9 us  [fused(): pl.pallas_call(functools.partial(fused_kernel, n_col), out_shape=[jax.Sha...]
    broadcast_in_dim x1 -> x0, local copies, waits for them, and re-layouts: 1.29 us -> none  [local(): vir_energy[None, :]]
where the time goes in v2:
time: 85 us; the launch traced here: 84.5 us
  Pallas kernels  80.9 us (95%)
  local copies, waits for them, and re-layouts  2.96 us (3%)
    pallas_call x1, Pallas kernels, fused(): pl.pallas_call(functools.partial(fused_kernel, n_col), out_shape=[jax.Sha...  80.9 us
    unnamed x2, local copies, waits for them, and re-layouts  2.96 us

profile of v2, /device:TPU:0, one launch (start us, length us, event | category | flops | bytes accessed | tf_op | source)
XLA Modules:
  0.0 84.5 jit_solution(292207302763442893)
XLA Ops:
  0.6 80.9 %shard_map.86 = (bf16[32,400]{1,0:T(8,128)(2,1)}, bf16[32,2400]{1,0:T(8,128)(2,1)}) custom-call(bf16[64,200]{1,0:T(8,128)(2,1)} %slab_occ.1, bf16[64,1200]{1,0:T(8,128)(2,1)} %slab_vir.1, bf16[200,1024]{1,0:T(8,128)(2,1)} %occ.1, bf16[1200,1024]{1,0:T(8,128)(2,1)} %vir.1, f32[200]{0:T(256)} %occ_energy.1, f32[1200]{0:T(1024)} %vir_energy.1, ...), custom_call_target="tpu_custom_call" | custom-call | tf_op jit(solution)/shard_map/pallas_call | solution.py:667
  81.5 1.4 %copy.11 = bf16[32,400]{1,0:T(8,128)(2,1)} copy(bf16[32,400]{1,0:T(8,128)(2,1)} %get-tuple-element.4) | data formatting | bytes 51200
  82.9 1.6 %copy.12 = bf16[32,2400]{1,0:T(8,128)(2,1)} copy(bf16[32,2400]{1,0:T(8,128)(2,1)} %get-tuple-element.5) | data formatting | bytes 307200

commit v3 on v2

--- a/solution.py
+++ b/solution.py
@@ -492,22 +492,27 @@
         def to_far(self, j):
             n = self.n
             self.second[j].wait_recv()
-            value = self.total[j] + wide(self.in_x[j])
-            if j == 0:
-                self.total[0] = value
-            else:
-                self.out_far[j - 1] = value.astype(kind)
-                push(self.out_far.at[j - 1], self.in_far.at[far], far_send.at[n, j - 1],
-                     far_recv.at[n, far], {"col": index(planes[j], mid, core)})
+            self.total[j] = self.total[j] + wide(self.in_x[j])
+            if j == n_far - 1:
+                pl.when(inner)(functools.partial(self.take, planes[2], j))
+            if j > 0:
+                self.out_far[j - 1] = self.total[j].astype(kind)
+                target, slot = planes[j], far
+                if j == 2:
+                    target = lax.select(inner, planes[2], planes[1])
+                    slot = lax.select(inner, far, planes[3])
+                push(self.out_far.at[j - 1], self.in_far.at[slot], far_send.at[n, j - 1],
+                     far_recv.at[n, slot], {"col": index(target, mid, core)})
+
+        def take(self, source, j):
+            landed(self.in_far.at[source], swap_send.at[0], far_recv.at[self.n, source], {"orb": other})
+            self.total[j] = self.total[j] + wide(self.in_far[source])
 
         def gather(self):
             n = self.n
-            value = self.total[0]
-            for j in range(1, n_far):
-                source = planes[j]
-                landed(self.in_far.at[source], swap_send.at[0], far_recv.at[n, source], {"orb": other})
-                value = value + wide(self.in_far[source])
-            self.total[0] = value
+            self.take(planes[1], 0)
+            pl.when(outer)(functools.partial(self.take, planes[2], 0))
+            self.take(planes[3], 0)
             lines = block // 2
             mine = pl.ds(pl.multiple_of(part * lines, lines), lines)
             theirs = pl.ds(pl.multiple_of(other * lines, lines), lines)
@@ -587,34 +592,34 @@
     project_vir(0)
     relay(1, 3, outer)
     cross(1, 2)
-    settle(1, 2)
     of_vir.to_mid(0)
     relay(0, 2, inner)
+    settle(1, 2)
     screened(2)
     make_side(2)
     cross(1, 3)
     relay(0, 2, outer)
     project_vir(1)
     of_vir.to_far(0)
-    of_vir.to_mid(1)
+    project_occ(0, mid)
     settle(1, 3)
     screened(3)
     make_side(3)
+    of_vir.to_mid(1)
     cross(0, 2)
     settle(0, 2)
     make_green(2)
     relay(0, 3, outer)
     project_vir(2)
+    project_occ(1)
     of_vir.to_far(1)
+    cross(0, 3)
     of_vir.to_mid(2)
-    cross(0, 3)
+    of_occ.to_mid(1)
     settle(0, 3)
     make_green(3)
     arrived(0, diagonal)
     make_green(0, other_mid)
-    project_occ(0, mid)
-    project_occ(1)
-    of_occ.to_mid(1)
     project_vir(3)
     of_vir.to_far(2)
     of_occ.to_far(1)
@@ -625,17 +630,17 @@
     project_occ(3)
     of_occ.to_far(2)
     of_occ.to_mid(3)
-    of_vir.gather()
     project_occ(0, other_mid)
     of_occ.to_mid(0)
     of_occ.to_far(3)
+    of_vir.gather()
+    of_occ.to_far(0)
+    of_occ.gather()
     low = part == 0
     own, peer = of_vir.end()
     own, peer = own[:, :n_vir], peer[:, :n_vir]
     out_vir[:, :n_vir] = jnp.where(low, own, peer).astype(kind)
     out_vir[:, n_vir:] = jnp.where(low, peer, own).astype(kind)
-    of_occ.to_far(0)
-    of_occ.gather()
     own, peer = of_occ.end()
     value = own + peer
     wide_occ = od.shape[1]
@@ -666,9 +671,7 @@
 
     return pl.pallas_call(
         functools.partial(fused_kernel, n_col),
-        out_shape=[
-            jax.ShapeDtypeStruct((block // 2, 2 * n), kind) for n in (n_occ, n_vir)
-        ],
+        out_shape=[pltpu.VMEM((block // 2, 2 * n), kind) for n in (n_occ, n_vir)],
         in_specs=[ANY] * 7,
         out_specs=[VMEM] * 2,
         scratch_shapes=[
@@ -701,7 +704,9 @@
             dma((2, n_far, 2)), dma((2, n_far, 2)), dma((2, n_far)), dma((2, n_far)),
             dma((2, n_far - 1)), dma((2, n_far)), dma((2,)), dma((2,)),
         ],
-        compiler_params=pltpu.CompilerParams(collective_id=2, has_side_effects=True),
+        compiler_params=pltpu.CompilerParams(
+            collective_id=2, has_side_effects=True, vmem_limit_bytes=60 * 2**20
+        ),
     )(slab_occ, slab_vir, occ, vir, occ_energy, vir_energy, screen)
 
 

time: 85 us -> 79.4 us (0.934)
  Pallas kernels: 80.9 us -> 77.2 us
  local copies, waits for them, and re-layouts: 2.96 us -> 1.28 us
    pallas_call x1, Pallas kernels: 80.9 us -> 77.2 us  [fused(): pl.pallas_call(functools.partial(fused_kernel, n_col), out_shape=[pltpu.V...]
    unnamed x2, local copies, waits for them, and re-layouts: 2.96 us -> 1.28 us
where the time goes in v3:
time: 79.4 us; the launch traced here: 79.2 us
  Pallas kernels  77.2 us (97%)
  local copies, waits for them, and re-layouts  1.28 us (2%)
    pallas_call x1, Pallas kernels, fused(): pl.pallas_call(functools.partial(fused_kernel, n_col), out_shape=[pltpu.V...  77.2 us

profile of v3, /device:TPU:0, one launch (start us, length us, event | category | flops | bytes accessed | tf_op | source)
XLA Modules:
  0.0 79.2 jit_solution(16275925702984873239)
XLA Ops:
  0.6 77.2 %shard_map.86 = (bf16[32,400]{1,0:T(8,128)(2,1)S(1)}, bf16[32,2400]{1,0:T(8,128)(2,1)S(1)}) custom-call(bf16[64,200]{1,0:T(8,128)(2,1)} %slab_occ.1, bf16[64,1200]{1,0:T(8,128)(2,1)} %slab_vir.1, bf16[200,1024]{1,0:T(8,128)(2,1)} %occ.1, bf16[1200,1024]{1,0:T(8,128)(2,1)} %vir.1, f32[200]{0:T(256)} %occ_energy.1, f32[1200]{0:T(1024)} %vir_energy.1, ...), custom_call_target="tpu_custom_call" | custom-call | tf_op jit(solution)/shard_map/pallas_call | solution.py:672
  77.9 0.6 copy.11
  78.5 0.7 copy.12

commit v4 on v3

--- a/solution.py
+++ b/solution.py
@@ -290,11 +290,12 @@
     out_occ, out_vir = refs[:2]
     (raw_occ, raw_vir, e_occ, e_vir, sv, so, ov, od, screens, green, green_out, green_in, side,
      part_vir, part_occ, near_vir, near_occ, out_x_vir, out_x_occ, in_x_vir, in_x_occ,
-     sum_vir, sum_occ, out_far_vir, out_far_occ, in_far_vir, in_far_occ,
-     end_out_vir, end_out_occ, end_in_vir, end_in_occ) = refs[2:33]
+     sum_vir, sum_occ, out_far_vir, out_far_occ, in_far_vir, joint_occ, in_far_occ, in_own_occ,
+     half_vir, half_occ, in_half_vir, in_half_occ, value_occ, in_last_vir) = refs[2:37]
     (load_sem, slab_send, slab_recv, swap_send, swap_recv, screen_send, screen_recv,
      green_send, green_recv, side_send, side_recv, near_send, near_recv, x_send, x_recv,
-     far_send, far_recv, end_send, end_recv) = refs[33:]
+     far_send, far_recv, half_send, half_recv, joint_send, joint_recv, occ_send, occ_recv,
+     own_send, own_recv, last_send, last_recv) = refs[37:]
     n_far = n_col // 4
     me, far, mid, core, index = place(n_col)
     part = lax.axis_index("orb")
@@ -324,7 +325,11 @@
         pl.semaphore_signal(
             barrier, inc=1, device_id={"col": lax.rem(me + d, n_col)}, device_id_type=MESH
         )
-    pl.semaphore_signal(barrier, inc=1, device_id={"orb": other}, device_id_type=MESH)
+    across = [me, x_peer, diagonal] + [index(f, mid, core) for f in planes[1:]]
+    for col in across:
+        pl.semaphore_signal(
+            barrier, inc=1, device_id={"col": col, "orb": other}, device_id_type=MESH
+        )
 
     def piece(p, k):
         start = p * (2 * half) + k * half
@@ -360,11 +365,11 @@
     so[me, part, :, :n_occ] = (wide(raw_occ[...]) * jnp.exp(e_occ[...])[None, :]).astype(kind)
     if so.shape[3] > n_occ:
         so[me, part, :, n_occ:] = jnp.zeros((block, so.shape[3] - n_occ), kind)
-    pl.semaphore_wait(barrier, n_col)
+    pl.semaphore_wait(barrier, n_col - 1 + len(across))
 
     sends = []
 
-    def push(src, dst, send, recv, device, only=None):
+    def push(src, dst, send, recv, device, only=None, shared=False):
         copy = pltpu.make_async_remote_copy(
             src_ref=src, dst_ref=dst, send_sem=send, recv_sem=recv,
             device_id=device, device_id_type=MESH,
@@ -373,16 +378,22 @@
             copy.start()
         else:
             pl.when(only)(copy.start)
-        sends.append((only, copy))
+        if not shared:
+            sends.append((only, copy))
         return copy
 
     slabs = (sv, so)
-    counter = [0]
-
-    def give(k, col, target, only=None):
-        push(slabs[k].at[col], slabs[k].at[col], slab_send.at[counter[0]], slab_recv.at[k, col],
-             {"col": target}, only)
-        counter[0] += 1
+
+    def give(k, col, target, only=None, chain=False):
+        push(slabs[k].at[col], slabs[k].at[col], slab_send.at[k, int(chain)], slab_recv.at[k, col],
+             {"col": target}, only, True)
+
+    def sent(ref, n, send):
+        ref = ref.at[pl.ds(0, n)]
+        pltpu.make_async_remote_copy(
+            src_ref=ref, dst_ref=ref, send_sem=send, recv_sem=swap_recv.at[0],
+            device_id={"orb": other}, device_id_type=MESH,
+        ).wait_send()
 
     def arrived(k, col, only=None):
         def act():
@@ -393,45 +404,43 @@
     def give_own(k):
         give(k, me, x_peer)
         give(k, me, index(planes[1], mid, core))
-        give(k, me, index(planes[3], mid, core), inner)
+        give(k, me, index(planes[3], mid, core), inner, True)
         give(k, me, core_peer)
 
     def relay(k, j, only=None):
         col = index(planes[j], mid, core)
         arrived(k, col, only)
         step = planes[3 if j == 1 else 1]
-        if only is not outer:
-            give(k, col, index(step, mid, core), inner)
+        if only is not outer and (k, j) != (0, 1):
+            give(k, col, index(step, mid, core), inner, True)
         give(k, col, x_peer, only)
         give(k, col, core_peer, only)
 
-    def cross(k, j):
+    def give_middle():
+        give(0, index(planes[1], mid, core), index(planes[3], mid, core), inner, True)
+
+    def cross(k, j, only=None):
         col = index(planes[j], 1 - mid, core)
-        arrived(k, col)
-        give(k, col, core_peer)
-
-    def settle(k, j):
-        arrived(k, index(planes[j], mid, 1 - core))
-        arrived(k, index(planes[j], 1 - mid, 1 - core))
-
-    screen_count = [0]
+        arrived(k, col, only)
+        give(k, col, core_peer, only)
+
+    def settle(k, j, only=None):
+        arrived(k, index(planes[j], mid, 1 - core), only)
+        arrived(k, index(planes[j], 1 - mid, 1 - core), only)
 
     def give_screen(target):
-        push(piece(target, part), screens.at[me], screen_send.at[screen_count[0]],
-             screen_recv.at[me], {"col": target})
-        screen_count[0] += 1
+        push(piece(target, part), screens.at[me], screen_send, screen_recv.at[far],
+             {"col": target}, None, True)
 
     def give_screens(j):
         for m, c in ((mid, core), (1 - mid, core), (mid, 1 - core), (1 - mid, 1 - core)):
             give_screen(index(planes[j], m, c))
 
     def screened(j):
-        for m, c in ((mid, core), (1 - mid, core), (mid, 1 - core), (1 - mid, 1 - core)):
-            if j == 0 and m is mid and c is core:
-                loads[7].wait()
-            else:
-                col = index(planes[j], m, c)
-                landed(screens.at[col], swap_send.at[0], screen_recv.at[col], {"orb": other})
+        if j == 0:
+            loads[7].wait()
+        ref = screens.at[pl.ds(planes[j] * 4, 4) if j else pl.ds(0, 3)]
+        landed(ref, swap_send.at[0], screen_recv.at[planes[j]], {"orb": other})
 
     def plane(j):
         return pl.ds(planes[j] * 4, 4)
@@ -445,16 +454,22 @@
     def chip(m):
         return pl.ds(planes[0] * 4 + 2 * m, 2), pl.ds(pl.multiple_of(m * (2 * block), 2 * block), 2 * block)
 
-    def make_green(j, m=None):
+    def when(only, act):
+        act() if only is None else pl.when(only)(act)
+
+    def make_green(j, m=None, only=None):
         owners, lines = (plane(j), pl.ds(0, rows)) if m is None else chip(m)
         slot = j if m is not other_mid else n_far
-        slab = sv[owners].reshape((-1, sv.shape[2]))
-        for cut in cuts:
-            green_out[j, lines, cut] = dot(slab, ov[other, :, cut]).astype(kind)
+
+        def fill(target, k, dtype):
+            slab = sv[owners].reshape((-1, sv.shape[2]))
+            for cut in cuts:
+                target[j, lines, cut] = dot(slab, ov[k, :, cut]).astype(dtype)
+
+        when(only, functools.partial(fill, green_out, other, kind))
         swaps["green", slot] = push(green_out.at[j, lines], green_in.at[j, lines], green_send.at[slot],
-                                    green_recv.at[slot], {"orb": other})
-        for cut in cuts:
-            green[j, lines, cut] = dot(slab, ov[part, :, cut])
+                                    green_recv.at[slot], {"orb": other}, only)
+        when(only, functools.partial(fill, green, part, jnp.float32))
 
     def make_side(j):
         for cut in cuts:
@@ -464,12 +479,15 @@
         swaps["side", j] = push(side.at[j, part], side.at[j, part], side_send.at[j],
                                 side_recv.at[j], {"orb": other})
 
+    lines = block // 2
+    mine = pl.ds(pl.multiple_of(part * lines, lines), lines)
+    theirs = pl.ds(pl.multiple_of(other * lines, lines), lines)
+
     class Reduce:
-        def __init__(self, n, part, near, out_x, in_x, total, out_far, in_far, end_out, end_in):
+        def __init__(self, n, part, near, out_x, in_x, total, out_far):
             self.n, self.part, self.near, self.out_x, self.in_x = n, part, near, out_x, in_x
-            self.total, self.out_far, self.in_far = total, out_far, in_far
-            self.end_out, self.end_in = end_out, end_in
-            self.first, self.second, self.third = {}, {}, {}
+            self.total, self.out_far = total, out_far
+            self.first, self.second = {}, {}
 
         def to_core(self, j, slots=(0, 1)):
             n = self.n
@@ -486,48 +504,110 @@
             self.out_x[j] = (wide(self.part[j, 1 - mid, core]) + wide(self.near[j, 0])).astype(kind)
             self.second[j] = push(self.out_x.at[j], self.in_x.at[j], x_send.at[n, j],
                                   x_recv.at[n, j], {"col": x_peer})
+            self.keep(j)
+
+        def keep(self, j):
             self.first[j, 1].wait_recv()
             self.total[j] = wide(self.part[j, mid, core]) + wide(self.near[j, 1])
 
-        def to_far(self, j):
-            n = self.n
+        def crossed(self, j):
             self.second[j].wait_recv()
             self.total[j] = self.total[j] + wide(self.in_x[j])
+
+    class ReduceVir(Reduce):
+        def to_far(self, j):
+            self.crossed(j)
             if j == n_far - 1:
                 pl.when(inner)(functools.partial(self.take, planes[2], j))
             if j > 0:
-                self.out_far[j - 1] = self.total[j].astype(kind)
+                out_far_vir[j - 1] = self.total[j].astype(kind)
                 target, slot = planes[j], far
+                if j == n_far - 1:
+                    col = index(target, mid, core)
+                    for n, (where, device) in enumerate(
+                        ((mine, {"col": col}), (theirs, {"col": col, "orb": other}))
+                    ):
+                        push(out_far_vir.at[j - 1, where], in_last_vir.at[part],
+                             last_send.at[n], last_recv.at[part], device)
+                    return
                 if j == 2:
                     target = lax.select(inner, planes[2], planes[1])
                     slot = lax.select(inner, far, planes[3])
-                push(self.out_far.at[j - 1], self.in_far.at[slot], far_send.at[n, j - 1],
-                     far_recv.at[n, slot], {"col": index(target, mid, core)})
+                push(out_far_vir.at[j - 1], in_far_vir.at[slot], far_send.at[j - 1],
+                     far_recv.at[slot], {"col": index(target, mid, core)})
 
         def take(self, source, j):
-            landed(self.in_far.at[source], swap_send.at[0], far_recv.at[self.n, source], {"orb": other})
-            self.total[j] = self.total[j] + wide(self.in_far[source])
+            landed(in_far_vir.at[source], swap_send.at[0], far_recv.at[source], {"orb": other})
+            self.total[j] = self.total[j] + wide(in_far_vir[source])
 
         def gather(self):
-            n = self.n
             self.take(planes[1], 0)
             pl.when(outer)(functools.partial(self.take, planes[2], 0))
-            self.take(planes[3], 0)
-            lines = block // 2
-            mine = pl.ds(pl.multiple_of(part * lines, lines), lines)
-            theirs = pl.ds(pl.multiple_of(other * lines, lines), lines)
-            self.end_out[...] = self.total[0, theirs].astype(kind)
-            self.last = push(self.end_out, self.end_in, end_send.at[n], end_recv.at[n], {"orb": other})
-            self.mine = mine
+            half_vir[...] = self.total[0, theirs].astype(kind)
+            self.last = push(half_vir, in_half_vir, half_send.at[0], half_recv.at[0], {"orb": other})
 
         def end(self):
             self.last.wait_recv()
-            return self.total[0, self.mine], wide(self.end_in[...])
-
-    of_vir = Reduce(0, part_vir, near_vir, out_x_vir, in_x_vir, sum_vir, out_far_vir, in_far_vir,
-                    end_out_vir, end_in_vir)
-    of_occ = Reduce(1, part_occ, near_occ, out_x_occ, in_x_occ, sum_occ, out_far_occ, in_far_occ,
-                    end_out_occ, end_in_occ)
+            for k in range(2):
+                landed(in_last_vir.at[k], swap_send.at[0], last_recv.at[k], {"orb": other})
+            own = self.total[0, mine] + wide(in_last_vir[part])
+            return own, wide(in_half_vir[...]) + wide(in_last_vir[other])
+
+    class ReduceOcc(Reduce):
+        def to_far(self, j):
+            self.crossed(j)
+            if j == n_far - 1:
+                pl.when(inner)(self.join)
+            out_far_occ[j - 1] = self.total[j].astype(kind)
+            col = index(planes[j], mid, core)
+            if j == 2:
+                self.joined = push(out_far_occ.at[1], joint_occ, joint_send, joint_recv,
+                                   {"col": index(planes[1], mid, core)}, outer)
+            for n, (where, device) in enumerate(
+                ((mine, {"col": col}), (theirs, {"col": col, "orb": other}))
+            ):
+                push(out_far_occ.at[j - 1, where], in_far_occ.at[far, part], far_send.at[n_far - 1 + 2 * (j - 1) + n],
+                     occ_recv.at[far, part], device, inner if j == 2 else None)
+
+        def join(self):
+            self.joined.wait_recv()
+            self.total[n_far - 1] = self.total[n_far - 1] + wide(joint_occ[...])
+
+        def own_half(self):
+            self.keep(0)
+            half_occ[...] = self.total[0, theirs].astype(kind)
+            self.last = push(half_occ, in_half_occ, half_send.at[1], half_recv.at[1], {"orb": other})
+
+        def direct(self):
+            n = 0
+            for c, col in ((core, x_peer), (1 - core, diagonal)):
+                for where, device in ((mine, {"col": col}), (theirs, {"col": col, "orb": other})):
+                    push(part_occ.at[0, other_mid, c, where], in_own_occ.at[core, part],
+                         own_send.at[n], own_recv.at[core, part], device)
+                    n += 1
+
+        def take(self, ref, recv):
+            landed(ref, swap_send.at[0], recv, {"orb": other})
+            value_occ[...] = value_occ[...] + wide(ref[...])
+
+        def take_far(self, source):
+            for k in range(2):
+                self.take(in_far_occ.at[source, k], occ_recv.at[source, k])
+
+        def collect(self):
+            self.last.wait_recv()
+            value_occ[...] = self.total[0, mine] + wide(in_half_occ[...])
+
+        def gather(self):
+            self.take_far(planes[1])
+            pl.when(outer)(functools.partial(self.take_far, planes[2]))
+            self.take_far(planes[3])
+            for c in range(2):
+                for k in range(2):
+                    self.take(in_own_occ.at[c, k], own_recv.at[c, k])
+
+    of_vir = ReduceVir(0, part_vir, near_vir, out_x_vir, in_x_vir, sum_vir, out_far_vir)
+    of_occ = ReduceOcc(1, part_occ, near_occ, out_x_occ, in_x_occ, sum_occ, out_far_occ)
 
     def project_vir(j):
         swaps["side", j].wait_recv()
@@ -553,7 +633,10 @@
                 part_occ[j, :, :, :, cut] = term
             else:
                 part_occ[j, m, :, :, cut] = term[0]
-        of_occ.to_core(j, (0, 1) if m is None else (0,) if m is other_mid else (1,))
+        if m is other_mid:
+            of_occ.direct()
+        else:
+            of_occ.to_core(j, (0, 1) if m is None else (1,))
 
     push(so.at[me, part], so.at[me, part], swap_send.at[0], swap_recv.at[0], {"orb": other})
     swap = push(columns_of(occ, other), od.at[part, pl.ds(0, n_occ)], swap_send.at[1],
@@ -589,63 +672,67 @@
     cross(0, 1)
     settle(0, 1)
     make_green(1)
+    give_middle()
     project_vir(0)
     relay(1, 3, outer)
     cross(1, 2)
+    project_occ(0, mid)
     of_vir.to_mid(0)
-    relay(0, 2, inner)
+    of_occ.own_half()
     settle(1, 2)
     screened(2)
     make_side(2)
     cross(1, 3)
     relay(0, 2, outer)
+    relay(0, 2, inner)
     project_vir(1)
-    of_vir.to_far(0)
-    project_occ(0, mid)
     settle(1, 3)
     screened(3)
     make_side(3)
     of_vir.to_mid(1)
     cross(0, 2)
+    of_vir.to_far(0)
     settle(0, 2)
     make_green(2)
     relay(0, 3, outer)
     project_vir(2)
     project_occ(1)
     of_vir.to_far(1)
-    cross(0, 3)
     of_vir.to_mid(2)
     of_occ.to_mid(1)
+    cross(0, 3)
     settle(0, 3)
     make_green(3)
     arrived(0, diagonal)
     make_green(0, other_mid)
     project_vir(3)
     of_vir.to_far(2)
-    of_occ.to_far(1)
     of_vir.to_mid(3)
     project_occ(2)
+    of_occ.to_far(1)
     of_occ.to_mid(2)
     of_vir.to_far(3)
     project_occ(3)
+    of_occ.to_mid(3)
     of_occ.to_far(2)
-    of_occ.to_mid(3)
     project_occ(0, other_mid)
-    of_occ.to_mid(0)
+    of_occ.collect()
+    of_vir.gather()
     of_occ.to_far(3)
-    of_vir.gather()
-    of_occ.to_far(0)
-    of_occ.gather()
     low = part == 0
     own, peer = of_vir.end()
     own, peer = own[:, :n_vir], peer[:, :n_vir]
     out_vir[:, :n_vir] = jnp.where(low, own, peer).astype(kind)
     out_vir[:, n_vir:] = jnp.where(low, peer, own).astype(kind)
-    own, peer = of_occ.end()
-    value = own + peer
+    of_occ.gather()
+    value = value_occ[...]
     wide_occ = od.shape[1]
     out_occ[:, :n_occ] = value[:, :n_occ].astype(kind)
     out_occ[:, n_occ:] = value[:, wide_occ : wide_occ + n_occ].astype(kind)
+    sent(screens, n_col - 1, screen_send)
+    for k in range(2):
+        sent(slabs[k], 3 + 2 * (n_far - 1) + n_far, slab_send.at[k, 0])
+        pl.when(inner)(functools.partial(sent, slabs[k], n_far, slab_send.at[k, 1]))
     for only, copy in sends:
         if only is None:
             copy.wait_send()
@@ -695,14 +782,21 @@
         + pair((n_far,), block)
         + pair((n_far,), block, f32)
         + pair((n_far - 1,), block)
-        + pair((n_far,), block)
+        + [
+            pltpu.VMEM((n_far, block, wide_vir), kind),
+            pltpu.VMEM((block, both), kind),
+            pltpu.VMEM((n_far, 2, block // 2, both), kind),
+            pltpu.VMEM((2, 2, block // 2, both), kind),
+        ]
         + pair((), block // 2)
         + pair((), block // 2)
+        + [pltpu.VMEM((block // 2, both), f32), pltpu.VMEM((2, block // 2, wide_vir), kind)]
         + [
-            dma((8,)), dma((42,)), dma((2, n_col)), dma((2,)), dma((2,)), dma((n_col,)), dma((n_col,)),
+            dma((8,)), dma((2, 2)), dma((2, n_col)), dma((2,)), dma((2,)), dma, dma((n_far,)),
             dma((n_far + 1,)), dma((n_far + 1,)), dma((n_far,)), dma((n_far,)),
             dma((2, n_far, 2)), dma((2, n_far, 2)), dma((2, n_far)), dma((2, n_far)),
-            dma((2, n_far - 1)), dma((2, n_far)), dma((2,)), dma((2,)),
+            dma((3 * (n_far - 1),)), dma((n_far,)), dma((2,)), dma((2,)), dma, dma,
+            dma((1,)), dma((n_far, 2)), dma((4,)), dma((2, 2)), dma((2,)), dma((2,)),
         ],
         compiler_params=pltpu.CompilerParams(
             collective_id=2, has_side_effects=True, vmem_limit_bytes=60 * 2**20

time: 79.4 us -> 77.2 us (0.972)
  Pallas kernels: 77.2 us -> 75.1 us
    pallas_call x1, Pallas kernels: 77.2 us -> 75.1 us  [fused(): pl.pallas_call(functools.partial(fused_kernel, n_col), out_shape=[pltpu.V...]
where the time goes in v4:
time: 77.2 us; the launch traced here: 77 us
  Pallas kernels  75.1 us (97%)
  local copies, waits for them, and re-layouts  1.28 us (2%)
    pallas_call x1, Pallas kernels, fused(): pl.pallas_call(functools.partial(fused_kernel, n_col), out_shape=[pltpu.V...  75.1 us

profile of v4, /device:TPU:0, one launch (start us, length us, event | category | flops | bytes accessed | tf_op | source)
XLA Modules:
  0.0 77.0 jit_solution(11131143250206818027)
XLA Ops:
  0.6 75.1 %shard_map.86 = (bf16[32,400]{1,0:T(8,128)(2,1)S(1)}, bf16[32,2400]{1,0:T(8,128)(2,1)S(1)}) custom-call(bf16[64,200]{1,0:T(8,128)(2,1)} %slab_occ.1, bf16[64,1200]{1,0:T(8,128)(2,1)} %slab_vir.1, bf16[200,1024]{1,0:T(8,128)(2,1)} %occ.1, bf16[1200,1024]{1,0:T(8,128)(2,1)} %vir.1, f32[200]{0:T(256)} %occ_energy.1, f32[1200]{0:T(1024)} %vir_energy.1, ...), custom_call_target="tpu_custom_call" | custom-call | tf_op jit(solution)/shard_map/pallas_call | solution.py:759
  75.8 0.6 copy.11
  76.4 0.7 copy.12

commit v5 on v4

--- a/solution.py
+++ b/solution.py
@@ -389,7 +389,7 @@
              {"col": target}, only, True)
 
     def sent(ref, n, send):
-        ref = ref.at[pl.ds(0, n)]
+        ref = ref if n is None else ref.at[pl.ds(0, n)]
         pltpu.make_async_remote_copy(
             src_ref=ref, dst_ref=ref, send_sem=send, recv_sem=swap_recv.at[0],
             device_id={"orb": other}, device_id_type=MESH,
@@ -432,6 +432,10 @@
         push(piece(target, part), screens.at[me], screen_send, screen_recv.at[far],
              {"col": target}, None, True)
 
+    def give_near():
+        for target in (x_peer, core_peer, diagonal):
+            give_screen(target)
+
     def give_screens(j):
         for m, c in ((mid, core), (1 - mid, core), (mid, 1 - core), (1 - mid, 1 - core)):
             give_screen(index(planes[j], m, c))
@@ -467,8 +471,8 @@
                 target[j, lines, cut] = dot(slab, ov[k, :, cut]).astype(dtype)
 
         when(only, functools.partial(fill, green_out, other, kind))
-        swaps["green", slot] = push(green_out.at[j, lines], green_in.at[j, lines], green_send.at[slot],
-                                    green_recv.at[slot], {"orb": other}, only)
+        swaps["green", slot] = push(green_out.at[j, lines], green_in.at[j, lines], green_send,
+                                    green_recv.at[slot], {"orb": other}, only, True)
         when(only, functools.partial(fill, green, part, jnp.float32))
 
     def make_side(j):
@@ -476,12 +480,17 @@
             value = dot(so[plane(j), 0].reshape((rows, -1)), od[0, :, cut])
             value = value + dot(so[plane(j), 1].reshape((rows, -1)), od[1, :, cut])
             side[j, part, :, cut] = (value * shade(j, cut)).astype(kind)
-        swaps["side", j] = push(side.at[j, part], side.at[j, part], side_send.at[j],
-                                side_recv.at[j], {"orb": other})
+        swaps["side", j] = push(side.at[j, part], side.at[j, part], side_send,
+                                side_recv.at[j], {"orb": other}, None, True)
 
     lines = block // 2
     mine = pl.ds(pl.multiple_of(part * lines, lines), lines)
     theirs = pl.ds(pl.multiple_of(other * lines, lines), lines)
+
+    def part_of(q, width):
+        if q < n_far - 1:
+            return q, pl.ds(0, width)
+        return n_far - 1, pl.ds((q - n_far + 1) * (width // 2), width // 2)
 
     class Reduce:
         def __init__(self, n, part, near, out_x, in_x, total, out_far):
@@ -489,46 +498,60 @@
             self.total, self.out_far = total, out_far
             self.first, self.second = {}, {}
 
-        def to_core(self, j, slots=(0, 1)):
+        def at(self, q):
+            return q, pl.ds(0, self.part.shape[-1])
+
+        def to_core(self, q, slots=(0, 1)):
             n = self.n
+            j, cut = self.at(q)
             for slot in slots:
                 m = (other_mid, mid)[slot]
-                self.first[j, slot] = push(
-                    self.part.at[j, m, 1 - core], self.near.at[j, slot],
-                    near_send.at[n, j, slot], near_recv.at[n, j, slot], {"col": core_peer},
+                self.first[q, slot] = push(
+                    self.part.at[j, m, 1 - core, :, cut], self.near.at[j, slot, :, cut],
+                    near_send.at[n], near_recv.at[n, q, slot], {"col": core_peer}, None, True,
                 )
 
-        def to_mid(self, j):
+        def to_mid(self, q):
             n = self.n
-            self.first[j, 0].wait_recv()
-            self.out_x[j] = (wide(self.part[j, 1 - mid, core]) + wide(self.near[j, 0])).astype(kind)
-            self.second[j] = push(self.out_x.at[j], self.in_x.at[j], x_send.at[n, j],
-                                  x_recv.at[n, j], {"col": x_peer})
-            self.keep(j)
-
-        def keep(self, j):
-            self.first[j, 1].wait_recv()
-            self.total[j] = wide(self.part[j, mid, core]) + wide(self.near[j, 1])
-
-        def crossed(self, j):
-            self.second[j].wait_recv()
-            self.total[j] = self.total[j] + wide(self.in_x[j])
+            j, cut = self.at(q)
+            self.first[q, 0].wait_recv()
+            self.out_x[j, :, cut] = (
+                wide(self.part[j, 1 - mid, core, :, cut]) + wide(self.near[j, 0, :, cut])
+            ).astype(kind)
+            self.second[q] = push(self.out_x.at[j, :, cut], self.in_x.at[j, :, cut], x_send.at[n],
+                                  x_recv.at[n, q], {"col": x_peer}, None, True)
+            self.keep(q)
+
+        def keep(self, q):
+            j, cut = self.at(q)
+            self.first[q, 1].wait_recv()
+            self.total[j, :, cut] = wide(self.part[j, mid, core, :, cut]) + wide(self.near[j, 1, :, cut])
+
+        def crossed(self, q):
+            j, cut = self.at(q)
+            self.second[q].wait_recv()
+            self.total[j, :, cut] = self.total[j, :, cut] + wide(self.in_x[j, :, cut])
 
     class ReduceVir(Reduce):
-        def to_far(self, j):
-            self.crossed(j)
+        def at(self, q):
+            return part_of(q, self.part.shape[-1])
+
+        def to_far(self, q):
+            j, cut = self.at(q)
+            self.crossed(q)
+            if q == n_far - 1:
+                pl.when(inner)(functools.partial(self.arrive, planes[2]))
             if j == n_far - 1:
-                pl.when(inner)(functools.partial(self.take, planes[2], j))
+                pl.when(inner)(functools.partial(self.add, planes[2], j, cut))
             if j > 0:
-                out_far_vir[j - 1] = self.total[j].astype(kind)
+                out_far_vir[j - 1, :, cut] = self.total[j, :, cut].astype(kind)
                 target, slot = planes[j], far
                 if j == n_far - 1:
                     col = index(target, mid, core)
-                    for n, (where, device) in enumerate(
-                        ((mine, {"col": col}), (theirs, {"col": col, "orb": other}))
-                    ):
-                        push(out_far_vir.at[j - 1, where], in_last_vir.at[part],
-                             last_send.at[n], last_recv.at[part], device)
+                    h = q - j
+                    for where, device in ((mine, {"col": col}), (theirs, {"col": col, "orb": other})):
+                        push(out_far_vir.at[j - 1, where, cut], in_last_vir.at[part, :, cut],
+                             last_send, last_recv.at[h, part], device, None, True)
                     return
                 if j == 2:
                     target = lax.select(inner, planes[2], planes[1])
@@ -536,20 +559,28 @@
                 push(out_far_vir.at[j - 1], in_far_vir.at[slot], far_send.at[j - 1],
                      far_recv.at[slot], {"col": index(target, mid, core)})
 
-        def take(self, source, j):
+        def arrive(self, source):
             landed(in_far_vir.at[source], swap_send.at[0], far_recv.at[source], {"orb": other})
-            self.total[j] = self.total[j] + wide(in_far_vir[source])
+
+        def add(self, source, j, cut):
+            self.total[j, :, cut] = self.total[j, :, cut] + wide(in_far_vir[source, :, cut])
+
+        def take(self, source):
+            self.arrive(source)
+            self.add(source, 0, pl.ds(0, self.part.shape[-1]))
 
         def gather(self):
-            self.take(planes[1], 0)
-            pl.when(outer)(functools.partial(self.take, planes[2], 0))
+            self.take(planes[1])
+            pl.when(outer)(functools.partial(self.take, planes[2]))
             half_vir[...] = self.total[0, theirs].astype(kind)
             self.last = push(half_vir, in_half_vir, half_send.at[0], half_recv.at[0], {"orb": other})
 
         def end(self):
             self.last.wait_recv()
-            for k in range(2):
-                landed(in_last_vir.at[k], swap_send.at[0], last_recv.at[k], {"orb": other})
+            for h in range(2):
+                cut = self.at(n_far - 1 + h)[1]
+                for k in range(2):
+                    landed(in_last_vir.at[k, :, cut], swap_send.at[0], last_recv.at[h, k], {"orb": other})
             own = self.total[0, mine] + wide(in_last_vir[part])
             return own, wide(in_half_vir[...]) + wide(in_last_vir[other])
 
@@ -579,12 +610,10 @@
             self.last = push(half_occ, in_half_occ, half_send.at[1], half_recv.at[1], {"orb": other})
 
         def direct(self):
-            n = 0
             for c, col in ((core, x_peer), (1 - core, diagonal)):
                 for where, device in ((mine, {"col": col}), (theirs, {"col": col, "orb": other})):
                     push(part_occ.at[0, other_mid, c, where], in_own_occ.at[core, part],
-                         own_send.at[n], own_recv.at[core, part], device)
-                    n += 1
+                         own_send, own_recv.at[core, part], device, None, True)
 
         def take(self, ref, recv):
             landed(ref, swap_send.at[0], recv, {"orb": other})
@@ -609,14 +638,18 @@
     of_vir = ReduceVir(0, part_vir, near_vir, out_x_vir, in_x_vir, sum_vir, out_far_vir)
     of_occ = ReduceOcc(1, part_occ, near_occ, out_x_occ, in_x_occ, sum_occ, out_far_occ)
 
-    def project_vir(j):
-        swaps["side", j].wait_recv()
-        width = part_vir.shape[-1]
-        for start in range(0, width, 256):
-            cut = slice(start, min(start + 256, width))
+    def project_vir(q):
+        j, _ = of_vir.at(q)
+        swap = swaps["side", j]
+        if q <= n_far - 1:
+            swap.wait_recv()
+        width = part_vir.shape[-1] // (1 if q < n_far - 1 else 2)
+        first = (q - j) * width
+        for start in range(first, first + width, 256):
+            cut = slice(start, min(start + 256, first + width))
             term = dot_t(side[j, 0], ov[0, cut]) + dot_t(side[j, 1], ov[1, cut])
             part_vir[j, :, :, :, cut] = term.astype(kind).reshape((2, 2, block, -1))
-        of_vir.to_core(j)
+        of_vir.to_core(q)
 
     def project_occ(j, m=None):
         slot = j if m is not other_mid else n_far
@@ -648,8 +681,7 @@
     make_green(0, mid)
     landed(so.at[me, other], swap_send.at[0], swap_recv.at[0], {"orb": other})
     give_own(1)
-    for target in (x_peer, core_peer, diagonal):
-        give_screen(target)
+    give_near()
     give_screens(1)
     cross(1, 0)
     relay(1, 1)
@@ -660,8 +692,8 @@
     screened(0)
     swap.wait_recv()
     make_side(0)
+    relay(1, 2, inner)
     cross(0, 0)
-    relay(1, 2, inner)
     give_screens(3)
     relay(0, 3, inner)
     cross(1, 1)
@@ -689,31 +721,34 @@
     settle(1, 3)
     screened(3)
     make_side(3)
+    cross(0, 2)
     of_vir.to_mid(1)
-    cross(0, 2)
     of_vir.to_far(0)
     settle(0, 2)
     make_green(2)
     relay(0, 3, outer)
     project_vir(2)
     project_occ(1)
-    of_vir.to_far(1)
     of_vir.to_mid(2)
     of_occ.to_mid(1)
     cross(0, 3)
     settle(0, 3)
     make_green(3)
     arrived(0, diagonal)
+    of_vir.to_far(1)
     make_green(0, other_mid)
     project_vir(3)
+    project_vir(4)
     of_vir.to_far(2)
     of_vir.to_mid(3)
+    of_vir.to_mid(4)
     project_occ(2)
-    of_occ.to_far(1)
     of_occ.to_mid(2)
     of_vir.to_far(3)
+    of_vir.to_far(4)
     project_occ(3)
     of_occ.to_mid(3)
+    of_occ.to_far(1)
     of_occ.to_far(2)
     project_occ(0, other_mid)
     of_occ.collect()
@@ -730,6 +765,14 @@
     out_occ[:, :n_occ] = value[:, :n_occ].astype(kind)
     out_occ[:, n_occ:] = value[:, wide_occ : wide_occ + n_occ].astype(kind)
     sent(screens, n_col - 1, screen_send)
+    sent(green_out, None, green_send)
+    sent(side, n_far // 2, side_send)
+    sent(near_vir, None, near_send.at[0])
+    sent(so, 2 * n_far - 1, near_send.at[1])
+    sent(out_x_vir, None, x_send.at[0])
+    sent(out_x_occ, n_far - 1, x_send.at[1])
+    sent(in_last_vir, None, last_send)
+    sent(in_own_occ, None, own_send)
     for k in range(2):
         sent(slabs[k], 3 + 2 * (n_far - 1) + n_far, slab_send.at[k, 0])
         pl.when(inner)(functools.partial(sent, slabs[k], n_far, slab_send.at[k, 1]))
@@ -793,10 +836,10 @@
         + [pltpu.VMEM((block // 2, both), f32), pltpu.VMEM((2, block // 2, wide_vir), kind)]
         + [
             dma((8,)), dma((2, 2)), dma((2, n_col)), dma((2,)), dma((2,)), dma, dma((n_far,)),
-            dma((n_far + 1,)), dma((n_far + 1,)), dma((n_far,)), dma((n_far,)),
-            dma((2, n_far, 2)), dma((2, n_far, 2)), dma((2, n_far)), dma((2, n_far)),
+            dma, dma((n_far + 1,)), dma, dma((n_far,)),
+            dma((2,)), dma((2, n_far + 1, 2)), dma((2,)), dma((2, n_far + 1)),
             dma((3 * (n_far - 1),)), dma((n_far,)), dma((2,)), dma((2,)), dma, dma,
-            dma((1,)), dma((n_far, 2)), dma((4,)), dma((2, 2)), dma((2,)), dma((2,)),
+            dma((1,)), dma((n_far, 2)), dma, dma((2, 2)), dma, dma((2, 2)),
         ],
         compiler_params=pltpu.CompilerParams(
             collective_id=2, has_side_effects=True, vmem_limit_bytes=60 * 2**20

time: 77.2 us -> 76.4 us (0.990)
  Pallas kernels: 75.1 us -> 74.2 us
    pallas_call x1, Pallas kernels: 75.1 us -> 74.2 us  [fused(): pl.pallas_call(functools.partial(fused_kernel, n_col), out_shape=[pltpu.V...]
where the time goes in v5:
time: 76.4 us; the launch traced here: 76.2 us
  Pallas kernels  74.2 us (97%)
  local copies, waits for them, and re-layouts  1.28 us (2%)
    pallas_call x1, Pallas kernels, fused(): pl.pallas_call(functools.partial(fused_kernel, n_col), out_shape=[pltpu.V...  74.2 us

profile of v5, /device:TPU:0, one launch (start us, length us, event | category | flops | bytes accessed | tf_op | source)
XLA Modules:
  0.0 76.2 jit_solution(9705991105944882788)
XLA Ops:
  0.6 74.2 %shard_map.86 = (bf16[32,400]{1,0:T(8,128)(2,1)S(1)}, bf16[32,2400]{1,0:T(8,128)(2,1)S(1)}) custom-call(bf16[64,200]{1,0:T(8,128)(2,1)} %slab_occ.1, bf16[64,1200]{1,0:T(8,128)(2,1)} %slab_vir.1, bf16[200,1024]{1,0:T(8,128)(2,1)} %occ.1, bf16[1200,1024]{1,0:T(8,128)(2,1)} %vir.1, f32[200]{0:T(256)} %occ_energy.1, f32[1200]{0:T(1024)} %vir_energy.1, ...), custom_call_target="tpu_custom_call" | custom-call | tf_op jit(solution)/shard_map/pallas_call | solution.py:802
  74.9 0.6 copy.11
  75.5 0.7 copy.12

commit v6 on v5

--- a/solution.py
+++ b/solution.py
@@ -734,14 +734,14 @@
     cross(0, 3)
     settle(0, 3)
     make_green(3)
-    arrived(0, diagonal)
     of_vir.to_far(1)
-    make_green(0, other_mid)
     project_vir(3)
     project_vir(4)
     of_vir.to_far(2)
     of_vir.to_mid(3)
     of_vir.to_mid(4)
+    arrived(0, diagonal)
+    make_green(0, other_mid)
     project_occ(2)
     of_occ.to_mid(2)
     of_vir.to_far(3)
@@ -847,6 +847,27 @@
     )(slab_occ, slab_vir, occ, vir, occ_energy, vir_energy, screen)
 
 
+def write_kernel(occ, vir, out_occ, out_vir, sem):
+    copies = [
+        pltpu.make_async_copy(src, dst, sem.at[n])
+        for n, (src, dst) in enumerate(((vir, out_vir), (occ, out_occ)))
+    ]
+    for copy in copies:
+        copy.start()
+    for copy in copies:
+        copy.wait()
+
+
+def settle_outputs(occ, vir):
+    return pl.pallas_call(
+        write_kernel,
+        out_shape=[jax.ShapeDtypeStruct(x.shape, x.dtype) for x in (occ, vir)],
+        in_specs=[VMEM] * 2,
+        out_specs=[ANY] * 2,
+        scratch_shapes=[pltpu.SemaphoreType.DMA((2,))],
+    )(*(pltpu.with_memory_space_constraint(x, pltpu.VMEM) for x in (occ, vir)))
+
+
 def local(slab_occ, slab_vir, orbitals_occ, orbitals_vir, occ_energy, vir_energy, screened):
     n_orb, n_col = lax.axis_size("orb"), lax.axis_size("col")
     part = lax.axis_index("orb")
@@ -856,9 +877,11 @@
     kind = slab_occ.dtype
     if n_col == 16 and n_orb == 2 and block % 16 == 0 and columns % 512 == 0:
         return tuple(
-            fused(
-                n_col, slab_occ, slab_vir, orbitals_occ, orbitals_vir,
-                occ_energy, vir_energy, screened,
+            settle_outputs(
+                *fused(
+                    n_col, slab_occ, slab_vir, orbitals_occ, orbitals_vir,
+                    occ_energy, vir_energy, screened,
+                )
             )
         )
     up = lambda n: -(-n // 128) * 128

time: 76.4 us -> 75.4 us (0.987)
  local copies, waits for them, and re-layouts: 1.28 us -> 0 us
    unnamed x2 -> x0, local copies, waits for them, and re-layouts: 1.28 us -> none
where the time goes in v6:
time: 75.4 us; the launch traced here: 75.2 us
  Pallas kernels  74.6 us (99%)
    pallas_call x1, Pallas kernels, fused(): pl.pallas_call(functools.partial(fused_kernel, n_col), out_shape=[pltpu.V...  73.9 us

profile of v6, /device:TPU:0, one launch (start us, length us, event | category | flops | bytes accessed | tf_op | source)
XLA Modules:
  0.0 75.2 jit_solution(4347017010224267710)
XLA Ops:
  0.6 73.9 %shard_map.86 = (bf16[32,400]{1,0:T(8,128)(2,1)S(1)}, bf16[32,2400]{1,0:T(8,128)(2,1)S(1)}) custom-call(bf16[64,200]{1,0:T(8,128)(2,1)} %slab_occ.1, bf16[64,1200]{1,0:T(8,128)(2,1)} %slab_vir.1, bf16[200,1024]{1,0:T(8,128)(2,1)} %occ.1, bf16[1200,1024]{1,0:T(8,128)(2,1)} %vir.1, f32[200]{0:T(256)} %occ_energy.1, f32[1200]{0:T(1024)} %vir_energy.1, ...), custom_call_target="tpu_custom_call" | custom-call | tf_op jit(solution)/shard_map/pallas_call | solution.py:802
  74.5 0.7 shard_map.87

commit v7 on v6

--- a/solution.py
+++ b/solution.py
@@ -325,7 +325,7 @@
         pl.semaphore_signal(
             barrier, inc=1, device_id={"col": lax.rem(me + d, n_col)}, device_id_type=MESH
         )
-    across = [me, x_peer, diagonal] + [index(f, mid, core) for f in planes[1:]]
+    across = [me, x_peer] + [index(f, mid, core) for f in planes[1:]]
     for col in across:
         pl.semaphore_signal(
             barrier, inc=1, device_id={"col": col, "orb": other}, device_id_type=MESH
@@ -609,11 +609,14 @@
             half_occ[...] = self.total[0, theirs].astype(kind)
             self.last = push(half_occ, in_half_occ, half_send.at[1], half_recv.at[1], {"orb": other})
 
-        def direct(self):
-            for c, col in ((core, x_peer), (1 - core, diagonal)):
-                for where, device in ((mine, {"col": col}), (theirs, {"col": col, "orb": other})):
-                    push(part_occ.at[0, other_mid, c, where], in_own_occ.at[core, part],
-                         own_send, own_recv.at[core, part], device, None, True)
+        def cross_own(self):
+            self.first[0, 0].wait_recv()
+            self.out_x[0] = (wide(self.part[0, other_mid, core]) + wide(self.near[0, 0])).astype(kind)
+            for where, device in (
+                (mine, {"col": x_peer}), (theirs, {"col": x_peer, "orb": other})
+            ):
+                push(self.out_x.at[0, where], in_own_occ.at[part], own_send, own_recv.at[part],
+                     device, None, True)
 
         def take(self, ref, recv):
             landed(ref, swap_send.at[0], recv, {"orb": other})
@@ -631,9 +634,8 @@
             self.take_far(planes[1])
             pl.when(outer)(functools.partial(self.take_far, planes[2]))
             self.take_far(planes[3])
-            for c in range(2):
-                for k in range(2):
-                    self.take(in_own_occ.at[c, k], own_recv.at[c, k])
+            for k in range(2):
+                self.take(in_own_occ.at[k], own_recv.at[k])
 
     of_vir = ReduceVir(0, part_vir, near_vir, out_x_vir, in_x_vir, sum_vir, out_far_vir)
     of_occ = ReduceOcc(1, part_occ, near_occ, out_x_occ, in_x_occ, sum_occ, out_far_occ)
@@ -666,10 +668,7 @@
                 part_occ[j, :, :, :, cut] = term
             else:
                 part_occ[j, m, :, :, cut] = term[0]
-        if m is other_mid:
-            of_occ.direct()
-        else:
-            of_occ.to_core(j, (0, 1) if m is None else (1,))
+        of_occ.to_core(j, (0, 1) if m is None else (0,) if m is other_mid else (1,))
 
     push(so.at[me, part], so.at[me, part], swap_send.at[0], swap_recv.at[0], {"orb": other})
     swap = push(columns_of(occ, other), od.at[part, pl.ds(0, n_occ)], swap_send.at[1],
@@ -753,6 +752,7 @@
     project_occ(0, other_mid)
     of_occ.collect()
     of_vir.gather()
+    of_occ.cross_own()
     of_occ.to_far(3)
     low = part == 0
     own, peer = of_vir.end()
@@ -768,7 +768,7 @@
     sent(green_out, None, green_send)
     sent(side, n_far // 2, side_send)
     sent(near_vir, None, near_send.at[0])
-    sent(so, 2 * n_far - 1, near_send.at[1])
+    sent(near_occ, None, near_send.at[1])
     sent(out_x_vir, None, x_send.at[0])
     sent(out_x_occ, n_far - 1, x_send.at[1])
     sent(in_last_vir, None, last_send)
@@ -829,7 +829,7 @@
             pltpu.VMEM((n_far, block, wide_vir), kind),
             pltpu.VMEM((block, both), kind),
             pltpu.VMEM((n_far, 2, block // 2, both), kind),
-            pltpu.VMEM((2, 2, block // 2, both), kind),
+            pltpu.VMEM((2, block // 2, both), kind),
         ]
         + pair((), block // 2)
         + pair((), block // 2)
@@ -839,7 +839,7 @@
             dma, dma((n_far + 1,)), dma, dma((n_far,)),
             dma((2,)), dma((2, n_far + 1, 2)), dma((2,)), dma((2, n_far + 1)),
             dma((3 * (n_far - 1),)), dma((n_far,)), dma((2,)), dma((2,)), dma, dma,
-            dma((1,)), dma((n_far, 2)), dma, dma((2, 2)), dma, dma((2, 2)),
+            dma((1,)), dma((n_far, 2)), dma, dma((2,)), dma, dma((2, 2)),
         ],
         compiler_params=pltpu.CompilerParams(
             collective_id=2, has_side_effects=True, vmem_limit_bytes=60 * 2**20

time: 75.4 us -> 75.4 us (level)
  no operation moved by 1% of the time
where the time goes in v7:
time: 75.4 us; the launch traced here: 75.2 us
  Pallas kernels  74.5 us (99%)
    pallas_call x1, Pallas kernels, fused(): pl.pallas_call(functools.partial(fused_kernel, n_col), out_shape=[pltpu.V...  73.8 us

profile of v7, /device:TPU:0, one launch (start us, length us, event | category | flops | bytes accessed | tf_op | source)
XLA Modules:
  0.0 75.2 jit_solution(2910100861577766349)
XLA Ops:
  0.6 73.8 %shard_map.86 = (bf16[32,400]{1,0:T(8,128)(2,1)S(1)}, bf16[32,2400]{1,0:T(8,128)(2,1)S(1)}) custom-call(bf16[64,200]{1,0:T(8,128)(2,1)} %slab_occ.1, bf16[64,1200]{1,0:T(8,128)(2,1)} %slab_vir.1, bf16[200,1024]{1,0:T(8,128)(2,1)} %occ.1, bf16[1200,1024]{1,0:T(8,128)(2,1)} %vir.1, f32[200]{0:T(256)} %occ_energy.1, f32[1200]{0:T(1024)} %vir_energy.1, ...), custom_call_target="tpu_custom_call" | custom-call | tf_op jit(solution)/shard_map/pallas_call | solution.py:802
  74.5 0.7 shard_map.87
